TPU v7x, 128 devices: a whole 4x4x4 slice. The times are simulated.
128 devices in a mesh: replica: 16 (over y_lo, z, core), tensor: 8 (over y_hi, x).
Axes of the slice: x: 4, y: 4 (y_hi: 2, y_lo: 2; y = y_hi * 2 + y_lo), z: 4, core: 2. Of those that a mesh axis runs over, the one named last changes fastest.
Arguments:
- hidden: bfloat16 [128, 2, 8192], P('replica'), may hold values from -6 to 6
- shard_rows: float32 [8704, 18432], P(('replica', 'tensor')), may hold values from -0.0625 to 0.0625
- piece_length: int32 [128], replicated, may hold values from 1 to 68, 8192 in all
- cache_keys: bfloat16 [128, 8, 4096, 128], P('replica', 'tensor'), may hold values from -200 to 200
- cache_values: bfloat16 [128, 8, 4096, 128], P('replica', 'tensor'), may hold values from -6 to 6
- cache_fill: int32 [128], P('replica'), may hold values from 1 to 4096, as said below
Outputs:
- layer_out: bfloat16 [128, 2, 8192], P('replica', None, 'tensor')
Inputs may be any that keep to these rules, and one draw needn't show every extreme that they name: `piece_length`: the device with replica index r and tensor index t holds piece r times the tensor axis size plus t; some piece has exactly 68 rows. `cache_fill`: some row has a full cache.
All inputs are finite; a program needn't handle non-finite values.
Results may differ from a plain program's by a relative error of at most 0.014.
Values may be sent and summed in bfloat16 or wider, within the bound.
No kernel may reach another device: no remote copies, remote signals or barrier semaphores. Data moves between devices by JAX's collectives and lax.ppermute only.
A program may use at most 192 MiB of HBM per device.

v0:
```python
import math

import jax
import jax.numpy as jnp
from jax import lax
from jax.sharding import PartitionSpec as P

D = 8192
HQ = 64
KV = 8
HD = 128


ROPE_BASE = 1000000.0
NEG_FILL = -1e30


def rotate(source, position):
    halfway = source.shape[-1] // 2
    exponent = jnp.arange(halfway, dtype=jnp.float32) * (2.0 / source.shape[-1])
    frequency = jnp.exp(-exponent * math.log(ROPE_BASE))
    angles = position[:, None, None] * frequency[None, None, :]
    cosine = jnp.cos(angles)
    sine_part = jnp.sin(angles)
    former = source[..., :halfway]
    latter = source[..., halfway:]
    return jnp.concatenate(
        [former * cosine - latter * sine_part, latter * cosine + former * sine_part], axis=-1
    )


def attend(projected, keys_cache, values_cache, filled):
    batch_rows, heads_kv, span_len, head_size = keys_cache.shape
    count = projected.shape[0]
    width_kv = heads_kv * head_size
    width_q = projected.shape[1] - 2 * width_kv
    heads_q = width_q // head_size
    group_size = heads_q // heads_kv
    position = (
        (filled[:, None] + jnp.arange(2, dtype=jnp.int32)[None, :]).reshape(-1).astype(jnp.float32)
    )
    query = rotate(projected[:, :width_q].reshape(count, heads_q, head_size), position).astype(
        jnp.bfloat16
    )
    new_key = rotate(
        projected[:, width_q : width_q + width_kv].reshape(count, heads_kv, head_size), position
    ).astype(jnp.bfloat16)
    new_value = (
        projected[:, width_q + width_kv :]
        .astype(jnp.bfloat16)
        .reshape(batch_rows, 2, heads_kv, head_size)
    )
    query = query.reshape(batch_rows, 2, heads_kv, group_size, head_size)
    new_key = new_key.reshape(batch_rows, 2, heads_kv, head_size)
    factor = 1.0 / math.sqrt(head_size)
    cached = (
        jnp.einsum("bskgd,bkcd->bkgsc", query, keys_cache, preferred_element_type=jnp.float32)
        * factor
    )
    recent = (
        jnp.einsum("bskgd,btkd->bkgst", query, new_key, preferred_element_type=jnp.float32) * factor
    )
    visible = (jnp.arange(span_len)[None, :] < filled[:, None])[:, None, None, None, :]
    causal = jnp.arange(2)[:, None] >= jnp.arange(2)[None, :]
    cached = jnp.where(visible, cached, NEG_FILL)
    recent = jnp.where(causal, recent, NEG_FILL)
    highest = jnp.maximum(jnp.max(cached, axis=-1), jnp.max(recent, axis=-1))
    cached_exp = jnp.exp(cached - highest[..., None])
    recent_exp = jnp.exp(recent - highest[..., None])
    total = jnp.sum(cached_exp, axis=-1) + jnp.sum(recent_exp, axis=-1)
    cached_prob = (cached_exp / total[..., None]).astype(jnp.bfloat16)
    recent_prob = (recent_exp / total[..., None]).astype(jnp.bfloat16)
    mixed = jnp.einsum(
        "bkgsc,bkcd->bskgd", cached_prob, values_cache, preferred_element_type=jnp.float32
    )
    mixed = mixed + jnp.einsum(
        "bkgst,btkd->bskgd", recent_prob, new_value, preferred_element_type=jnp.float32
    )
    return mixed.astype(jnp.bfloat16).reshape(count, width_q)


def split_slices(block, slices, width_q, width_kv):
    height = block.shape[0]
    bounds = (0, width_q, width_q + width_kv, width_q + 2 * width_kv, block.shape[1])
    pieces = [
        block[:, bounds[index] : bounds[index + 1]].reshape(height, slices, -1)
        for index in range(4)
    ]
    return jnp.concatenate(pieces, axis=2).astype(jnp.bfloat16)


def padded_columns(matrix, piece_length, starts, capacity):
    offsets = jnp.arange(capacity, dtype=jnp.int32)
    source = (starts[:, None] + offsets[None, :]).reshape(-1)
    valid = (offsets[None, :] < piece_length[:, None]).reshape(-1)
    source = jnp.clip(source, 0, matrix.shape[1] - 1)
    picked = jnp.take(matrix, source, axis=1)
    return jnp.where(valid[None, :], picked, jnp.zeros((), matrix.dtype))


def model_order(padded, piece_ends, starts, capacity):
    global_row = jnp.arange(D, dtype=jnp.int32)
    passed = piece_ends[None, :] <= global_row[:, None]
    owners = jnp.sum(passed.astype(jnp.int32), axis=1)
    own_start = jnp.max(
        jnp.where(starts[None, :] <= global_row[:, None], starts[None, :], 0), axis=1
    )
    source = owners * capacity + (global_row - own_start)
    return jnp.take(padded, source, axis=1)


def body(hidden, shard_rows, piece_length, cache_keys, cache_values, cache_fill):
    slices = lax.axis_size("tensor")
    capacity = shard_rows.shape[0]
    batch_rows = cache_keys.shape[0]
    project_width = (HQ + 2 * KV) * HD // slices
    tokens = hidden.reshape(batch_rows * 2, hidden.shape[2])
    stacked = split_slices(shard_rows, slices, HQ * HD, KV * HD)
    received = lax.all_to_all(stacked, "tensor", split_axis=1, concat_axis=0, tiled=True).reshape(
        slices * capacity, -1
    )
    piece_ends = jnp.cumsum(piece_length)
    starts = piece_ends - piece_length
    gathered = lax.all_gather(received, "replica", axis=0, tiled=True)
    token_cols = padded_columns(tokens, piece_length, starts, capacity)
    projected = jnp.dot(token_cols, gathered[:, :project_width], preferred_element_type=jnp.float32)
    attended = attend(projected, cache_keys, cache_values, cache_fill)
    padded_out = jnp.einsum(
        "tf,jf->tj", attended, gathered[:, project_width:], preferred_element_type=jnp.float32
    )
    partial_value = model_order(padded_out, piece_ends, starts, capacity)
    result = lax.psum_scatter(
        partial_value.astype(jnp.bfloat16), "tensor", scatter_dimension=1, tiled=True
    )
    return result.reshape(batch_rows, 2, -1)


def solution(mesh):
    placed = (
        P("replica", None, None),
        P(("replica", "tensor"), None),
        P(),
        P("replica", "tensor", None, None),
        P("replica", "tensor", None, None),
        P("replica"),
    )
    return jax.shard_map(
        body, mesh=mesh, in_specs=placed, out_specs=P("replica", None, "tensor"), check_vma=False
    )
```

profile of v0, /device:TPU:0, one launch (start us, length us, event | category | flops | bytes accessed | tf_op | source)
XLA Modules:
  0.0 405.0 jit_solution(11453051769635122451)
XLA Ops:
  6.5 2.8 convert.33
  9.5 0.7 copy.32
  10.3 0.6 copy.21
  10.9 0.7 copy.35
  11.7 0.6 copy.24
  12.5 0.2 pad_maximum_fusion
  12.7 41.8 %all_to_all.15 = bf16[68,8,2304]{2,0,1:T(8,128)(2,1)S(1)} all-to-all(bf16[68,8,2304]{2,0,1:T(8,128)(2,1)S(1)} %pad_maximum_fusion), channel_id=1, replica_groups=mesh['replica'=16,'tensor'=8] {'tensor'}, dimensions={1} | all-to-all | bytes 5013504 | tf_op jit(solution)/shard_map/all_to_all | solution.py:119
  54.5 2.2 reshape.409
  56.9 0.6 copy-done.1
  58.3 1.0 copy.20
  59.8 18.3 %gather_fusion = bf16[8704,16]{1,0:T(8,128)(2,1)} fusion(bf16[16,8192]{0,1:T(8,128)(2,1)S(1)} %copy.20, s32[9216]{0:T(1024)S(1)} %pad_clamp_fusion), kind=kCustom, calls=%fused_computation | custom fusion | bytes 591872 | tf_op jit(solution)/shard_map/jit(_take)/gather | solution.py:97
  78.3 2.2 select_reduce_fusion
  80.8 175.7 %all-gather.2.cloned.1.call-done = bf16[8704,2304]{1,0:T(8,128)(2,1)} async-done(((bf16[544,2304]{1,0:T(8,128)(2,1)}), bf16[8704,2304]{1,0:T(8,128)(2,1)}) %all-gather.2.cloned.1.call-update) | async-done | bytes 40108048 | tf_op jit(solution)/shard_map/all_gather | solution.py:124
  256.5 10.1 %fusion = f32[16,1280]{1,0:T(8,128)S(1)} fusion(bf16[8704,2304]{1,0:T(8,128)(2,1)} %all-gather.2.cloned.1.call-done, bf16[8704,16]{1,0:T(8,128)(2,1)} %gather_fusion, pred[8704]{0:T(1024)(128)(4,1)S(1)} %lt.85, pred[8704]{0:T(1024)(128)(4,1)S(1)} %compare_and_fusion), kind=kOutput, calls=%fused_computation.2 | convolution fusion | flops 356794368 | bytes 24609792 | tf_op jit(solution)/shard_map/dot_general | solution.py:126
  266.9 5.8 %fusion.58 = (f32[8,8,2]{1,2,0:T(2,128)S(1)}, f32[8,1,8,2,4096]{4,2,3,0,1:T(8,128)S(1)}) fusion(bf16[8,1,4096,128]{3,2,1,0:T(8,128)(2,1)} %param.9, bf16[8,2,8,64]{3,2,1,0:T(8,128)(2,1)S(1)} %bitcast.115, bf16[8,2,8,64]{3,2,1,0:T(8,128)(2,1)S(1)} %bitcast.113, pred[8,4096]{1,0:T(8,128)(4,1)S(1)} %iota_compare_fusion.2), kind=kOutput, calls=%fused_computation.88 | convolution fusion | flops 135856000 | bytes 10551808 | tf_op jit(solution)/shard_map/bskgd,bkcd->bkgsc/dot_general | solution.py:57
  272.7 0.4 fusion.59
  273.1 0.4 fusion.25
  273.5 4.7 %fusion.26 = f32[8,128,8,2]{1,2,3,0:T(8,128)S(1)} fusion(bf16[8,1,4096,128]{3,2,1,0:T(8,128)(2,1)} %param.10, f32[8,1,8,2,4096]{4,2,3,0,1:T(8,128)S(1)} %get-tuple-element.16, f32[8,8,2]{1,2,0:T(2,128)S(1)} %add.134, f32[8,8,2]{1,2,0:T(2,128)S(1)} %max.22), kind=kOutput, calls=%fused_computation.28 | convolution fusion | flops 135790592 | bytes 10552320 | tf_op jit(solution)/shard_map/bkgsc,bkcd->bskgd/dot_general | solution.py:73
  278.5 12.5 %fusion.2 = bf16[16,8704]{0,1:T(8,128)(2,1)} fusion(bf16[8704,2304]{1,0:T(8,128)(2,1)} %all-gather.2.cloned.1.call-done, bf16[2,8,8,128]{3,2,1,0:T(8,128)(2,1)S(1)} %bitcast.123), kind=kOutput, calls=%fused_computation.4 | convolution fusion | flops 285212672 | bytes 18137088 | tf_op jit(solution)/shard_map/tf,jf->tj/dot_general | solution.py:128
  291.0 23.8 %gather_fusion.1 = bf16[8192,16]{1,0:T(8,128)(2,1)S(1)} fusion(bf16[16,8704]{0,1:T(8,128)(2,1)} %fusion.2, s32[8192]{0:T(1024)S(1)} %broadcast_clamp_fusion), kind=kCustom, calls=%fused_computation.1 | custom fusion | bytes 557056 | tf_op jit(solution)/shard_map/jit(_take)/gather | solution.py:109
  314.8 5.0 %fusion.24 = bf16[16,8192]{0,1:T(8,128)(2,1)} fusion(bf16[8192,16]{1,0:T(8,128)(2,1)S(1)} %gather_fusion.1, pred[8192]{0:T(1024)(128)(4,1)S(1)} %compare_and_fusion.1), kind=kLoop, calls=%fused_computation.24 | loop fusion | flops 131072 | bytes 532480 | tf_op jit(solution)/shard_map/convert_element_type | solution.py:133
  319.9 76.5 %reduce-scatter.2.cloned.1.call-done = bf16[16,1024]{0,1:T(8,128)(2,1)} async-done(((bf16[16,8192]{0,1:T(8,128)(2,1)}), bf16[16,1024]{0,1:T(8,128)(2,1)}) %reduce-scatter.2.cloned.1.call-update) | async-done | bytes 32784 | tf_op jit(solution)/shard_map/reduce_scatter | solution.py:132
  396.4 1.0 copy.26
  397.5 0.6 reshape.418
  (52 shorter events, 2.7 us)
Async XLA Ops:
  6.5 250.0 %all-gather.2.cloned.1.call-start = ((), (), s32[]{:S(2)}) async-start(), calls=%async_computation.2 | async-start | bytes 42614784 | tf_op jit(solution)/shard_map/all_gather | solution.py:124
  56.8 0.7 copy-start.1
  56.8 1.4 copy-start
  56.8 2.7 copy-start.2
  56.8 339.6 %reduce-scatter.2.cloned.1.call-start = ((), (), s32[]{:S(2)}) async-start(), calls=%async_computation.3 | async-start | bytes 2359296 | tf_op jit(solution)/shard_map/reduce_scatter | solution.py:132
Sparse Core Ops, SparseCore 0:
  56.9 199.5 all-gather.1
  320.0 76.3 reduce-scatter.1
where the time goes:
time: 405 us
  waiting for transfers between devices  252 us (62%)
  local copies, waits for them, and re-layouts  51.4 us (13%)
  blocking collectives  41.8 us (10%)
  matrix products  33.7 us (8%)
  between operations  13.8 us (3%)
  other arithmetic  12 us (3%)
    all_gather x1, waiting for transfers between devices, body(): gathered = lax.all_gather(received, 'replica', axis=0, tiled=True)  176 us
    reduce_scatter x1, waiting for transfers between devices, body(): lax.psum_scatter(partial_value.astype(jnp.bfloat16), 'tensor', scatter_di...  76.5 us
    all_to_all x1, blocking collectives, body(): lax.all_to_all(stacked, 'tensor', split_axis=1, concat_axis=0, tiled=True)  41.8 us
    gather x1, local copies, waits for them, and re-layouts, model_order(): return jnp.take(padded, source, axis=1)  23.8 us
    gather x1, local copies, waits for them, and re-layouts, padded_columns(): picked = jnp.take(matrix, source, axis=1)  18.3 us
    dot_general x1, matrix products, body(): jnp.einsum('tf,jf->tj', attended, gathered[:, project_width:], preferred_...  12.5 us
    dot_general x1, matrix products, body(): jnp.dot(token_cols, gathered[:, :project_width], preferred_element_type=j...  10.1 us
  transfers between devices with their start and end apart: 2, of which 2 were waited for; matrix products, arithmetic and copies ran while one was open for 6% of the time, Pallas kernels for 0%

commit v1 on v0

v1 whole, which is shorter than its diff:
```python
import math

import jax
import jax.numpy as jnp
from jax import lax
from jax.experimental import pallas as pl
from jax.experimental.pallas import tpu as pltpu
from jax.sharding import PartitionSpec as P

D = 8192
HQ = 64
KV = 8
HD = 128
ROPE_BASE = 1000000.0
NEG_FILL = -1e30
ROWS = 72
WINDOW = 768
LANES = 128


def rope_tables(position):
    halfway = HD // 2
    exponent = jnp.arange(halfway, dtype=jnp.float32) * (2.0 / HD)
    frequency = jnp.exp(-exponent * math.log(ROPE_BASE))
    angles = position[:, None] * frequency[None, :]
    return jnp.cos(angles), jnp.sin(angles)


def rotate(source, cosine, sine_part):
    halfway = source.shape[-1] // 2
    former = source[..., :halfway]
    latter = source[..., halfway:]
    return jnp.concatenate(
        [former * cosine - latter * sine_part, latter * cosine + former * sine_part], axis=-1
    )


def attend(projected, keys_cache, values_cache, filled, cosine, sine_part):
    batch_rows, heads_kv, span_len, head_size = keys_cache.shape
    count = projected.shape[0]
    width_kv = heads_kv * head_size
    width_q = projected.shape[1] - 2 * width_kv
    heads_q = width_q // head_size
    group_size = heads_q // heads_kv
    cosine = cosine[:, None, :]
    sine_part = sine_part[:, None, :]
    query = rotate(
        projected[:, :width_q].reshape(count, heads_q, head_size), cosine, sine_part
    ).astype(jnp.bfloat16)
    new_key = rotate(
        projected[:, width_q : width_q + width_kv].reshape(count, heads_kv, head_size),
        cosine,
        sine_part,
    ).astype(jnp.bfloat16)
    new_value = (
        projected[:, width_q + width_kv :]
        .astype(jnp.bfloat16)
        .reshape(batch_rows, 2, heads_kv, head_size)
    )
    query = query.reshape(batch_rows, 2, heads_kv, group_size, head_size)
    new_key = new_key.reshape(batch_rows, 2, heads_kv, head_size)
    factor = 1.0 / math.sqrt(head_size)
    cached = (
        jnp.einsum("bskgd,bkcd->bkgsc", query, keys_cache, preferred_element_type=jnp.float32)
        * factor
    )
    recent = (
        jnp.einsum("bskgd,btkd->bkgst", query, new_key, preferred_element_type=jnp.float32) * factor
    )
    visible = (jnp.arange(span_len)[None, :] < filled[:, None])[:, None, None, None, :]
    causal = jnp.arange(2)[:, None] >= jnp.arange(2)[None, :]
    cached = jnp.where(visible, cached, NEG_FILL)
    recent = jnp.where(causal, recent, NEG_FILL)
    highest = jnp.maximum(jnp.max(cached, axis=-1), jnp.max(recent, axis=-1))
    cached_exp = jnp.exp(cached - highest[..., None])
    recent_exp = jnp.exp(recent - highest[..., None])
    total = jnp.sum(cached_exp, axis=-1) + jnp.sum(recent_exp, axis=-1)
    cached_prob = (cached_exp / total[..., None]).astype(jnp.bfloat16)
    recent_prob = (recent_exp / total[..., None]).astype(jnp.bfloat16)
    mixed = jnp.einsum(
        "bkgsc,bkcd->bskgd", cached_prob, values_cache, preferred_element_type=jnp.float32
    )
    mixed = mixed + jnp.einsum(
        "bkgst,btkd->bskgd", recent_prob, new_value, preferred_element_type=jnp.float32
    )
    return mixed.astype(jnp.bfloat16).reshape(count, width_q)


def slice_body(q_ref, k_ref, v_ref, o_ref, in_ref, out_ref):
    height = q_ref.shape[0]
    qw, kw = q_ref.shape[1], k_ref.shape[1]
    in_ref[0, 0:height, 0:qw] = q_ref[...].astype(jnp.bfloat16)
    in_ref[0, 0:height, qw : qw + kw] = k_ref[...].astype(jnp.bfloat16)
    in_ref[0, 0:height, qw + kw : qw + 2 * kw] = v_ref[...].astype(jnp.bfloat16)
    in_ref[0, height:ROWS, :] = jnp.zeros((ROWS - height, qw + 2 * kw), jnp.bfloat16)
    out_ref[0, 0:height, :] = o_ref[...].astype(jnp.bfloat16)
    out_ref[0, height:ROWS, :] = jnp.zeros((ROWS - height, qw), jnp.bfloat16)


def split_slices(block, slices):
    height = block.shape[0]
    qw = HQ * HD // slices
    kw = KV * HD // slices
    project = (HQ + 2 * KV) * HD
    return pl.pallas_call(
        slice_body,
        grid=(slices,),
        in_specs=[
            pl.BlockSpec((height, qw), lambda t: (0, t)),
            pl.BlockSpec((height, kw), lambda t: (0, HQ * HD // kw + t)),
            pl.BlockSpec((height, kw), lambda t: (0, (HQ + KV) * HD // kw + t)),
            pl.BlockSpec((height, qw), lambda t: (0, project // qw + t)),
        ],
        out_specs=[
            pl.BlockSpec((1, ROWS, qw + 2 * kw), lambda t: (t, 0, 0)),
            pl.BlockSpec((1, ROWS, qw), lambda t: (t, 0, 0)),
        ],
        out_shape=[
            jax.ShapeDtypeStruct((slices, ROWS, qw + 2 * kw), jnp.bfloat16),
            jax.ShapeDtypeStruct((slices, ROWS, qw), jnp.bfloat16),
        ],
        name="split_slices",
    )(block, block, block, block)


def windows_body(first_ref, tokens_ref, out_ref):
    for index in range(out_ref.shape[0]):
        first = pl.multiple_of(first_ref[index], LANES)
        out_ref[index] = tokens_ref[:, pl.ds(first, WINDOW)]


def token_windows(tokens, first):
    return pl.pallas_call(
        windows_body,
        in_specs=[
            pl.BlockSpec(memory_space=pltpu.SMEM),
            pl.BlockSpec(memory_space=pltpu.VMEM),
        ],
        out_specs=pl.BlockSpec(memory_space=pltpu.VMEM),
        out_shape=jax.ShapeDtypeStruct((first.shape[0], tokens.shape[0], WINDOW), tokens.dtype),
        name="token_windows",
    )(first, tokens)


def place_body(first_ref, part_ref, out_ref, acc_ref):
    acc_ref[...] = jnp.zeros_like(acc_ref)
    for index in range(part_ref.shape[0]):
        first = pl.multiple_of(first_ref[index], LANES)
        acc_ref[:, pl.ds(first, WINDOW)] = acc_ref[:, pl.ds(first, WINDOW)] + part_ref[
            index
        ].astype(jnp.float32)
    width = out_ref.shape[2]
    for index in range(out_ref.shape[0]):
        out_ref[index] = acc_ref[:, index * width : (index + 1) * width].astype(out_ref.dtype)


def place_windows(parts, first, slices):
    count = parts.shape[1]
    return pl.pallas_call(
        place_body,
        in_specs=[
            pl.BlockSpec(memory_space=pltpu.SMEM),
            pl.BlockSpec(memory_space=pltpu.VMEM),
        ],
        out_specs=pl.BlockSpec(memory_space=pltpu.VMEM),
        out_shape=jax.ShapeDtypeStruct((slices, count, D // slices), parts.dtype),
        scratch_shapes=[pltpu.VMEM((count, D), jnp.float32)],
        name="place_windows",
    )(first, parts)


def body(hidden, shard_rows, piece_length, cache_keys, cache_values, cache_fill):
    slices = lax.axis_size("tensor")
    replicas = lax.axis_size("replica")
    replica = lax.axis_index("replica")
    batch_rows = cache_keys.shape[0]
    count = batch_rows * 2
    tokens = hidden.reshape(count, hidden.shape[2])

    piece_ends = jnp.cumsum(piece_length)
    starts = piece_ends - piece_length
    by_replica = starts.reshape(replicas, slices)
    first = jnp.minimum(by_replica[:, 0] // LANES * LANES, D - WINDOW).astype(jnp.int32)
    own_starts = lax.dynamic_index_in_dim(by_replica, replica, 0, keepdims=False)
    own_length = lax.dynamic_index_in_dim(
        piece_length.reshape(replicas, slices), replica, 0, keepdims=False
    )
    own_first = lax.dynamic_index_in_dim(first, replica, 0, keepdims=False)
    offsets = jnp.arange(ROWS, dtype=jnp.int32)
    target = jnp.where(
        offsets[None, :] < own_length[:, None], own_starts[:, None] + offsets[None, :] - own_first, -1
    ).reshape(-1)
    choose = (jnp.arange(WINDOW, dtype=jnp.int32)[:, None] == target[None, :]).astype(jnp.bfloat16)

    project_rows, output_rows = split_slices(shard_rows, slices)
    token_parts = token_windows(tokens, first)
    project_rows = lax.all_to_all(project_rows, "tensor", split_axis=0, concat_axis=0, tiled=True)
    token_parts = lax.all_to_all(token_parts, "replica", split_axis=0, concat_axis=0, tiled=True)
    output_rows = lax.all_to_all(output_rows, "tensor", split_axis=0, concat_axis=0, tiled=True)
    project_rows = project_rows.reshape(slices * ROWS, -1)
    output_rows = output_rows.reshape(slices * ROWS, -1)

    own_tokens = jnp.dot(
        token_parts.reshape(replicas * count, WINDOW), choose, preferred_element_type=jnp.float32
    ).astype(jnp.bfloat16)
    partial = jnp.dot(own_tokens, project_rows, preferred_element_type=jnp.float32)
    partial = partial.astype(jnp.bfloat16).reshape(replicas, count, -1)
    partial = lax.all_to_all(partial, "replica", split_axis=0, concat_axis=0, tiled=True)
    projected = jnp.sum(partial.astype(jnp.float32), axis=0)

    position = (
        (cache_fill[:, None] + jnp.arange(2, dtype=jnp.int32)[None, :])
        .reshape(-1)
        .astype(jnp.float32)
    )
    cosine, sine_part = rope_tables(position)
    attended = attend(projected, cache_keys, cache_values, cache_fill, cosine, sine_part)
    gathered = lax.all_gather(attended, "replica", axis=0, tiled=True)
    output_window = jnp.dot(choose, output_rows, preferred_element_type=jnp.float32).astype(
        jnp.bfloat16
    )
    parts = lax.dot_general(
        gathered, output_window, (((1,), (1,)), ((), ())), preferred_element_type=jnp.float32
    )
    parts = parts.astype(jnp.bfloat16).reshape(replicas, count, WINDOW)
    parts = lax.all_to_all(parts, "replica", split_axis=0, concat_axis=0, tiled=True)
    placed = place_windows(parts, first, slices)
    placed = lax.all_to_all(placed, "tensor", split_axis=0, concat_axis=0, tiled=True)
    result = jnp.sum(placed.astype(jnp.float32), axis=0).astype(jnp.bfloat16)
    return result.reshape(batch_rows, 2, -1)


def solution(mesh):
    placed = (
        P("replica", None, None),
        P(("replica", "tensor"), None),
        P(),
        P("replica", "tensor", None, None),
        P("replica", "tensor", None, None),
        P("replica"),
    )
    return jax.shard_map(
        body, mesh=mesh, in_specs=placed, out_specs=P("replica", None, "tensor"), check_vma=False
    )
```

time: 405 us -> 136 us (0.34)
  waiting for transfers between devices: 252 us -> 34.7 us
  local copies, waits for them, and re-layouts: 51.4 us -> 4.21 us
  starting transfers between devices: 0.04 us -> 20.4 us
  matrix products: 33.7 us -> 14.8 us
  between operations: 13.8 us -> 0.18 us
  Pallas kernels: 0 us -> 10.2 us
  other arithmetic: 12 us -> 3.25 us
  blocking collectives: 41.8 us -> 47.4 us
    all_gather x1 -> x0, waiting for transfers between devices: 176 us -> none  [body(): gathered = lax.all_gather(received, 'replica', axis=0, tiled=True)]
    reduce_scatter x1 -> x0, waiting for transfers between devices: 76.5 us -> none  [body(): lax.psum_scatter(partial_value.astype(jnp.bfloat16), 'tensor', scatter_di...]
    gather x2 -> x0, local copies, waits for them, and re-layouts: 42.2 us -> none  [the longest x1 23.8 us: model_order(): return jnp.take(padded, source, axis=1)]
    all_to_all x0 -> x4, waiting for transfers between devices: none -> 34.7 us  [the longest x1 19.6 us: body(): lax.all_to_all(project_rows, 'tensor', split_axis=0, concat_axis=0, tiled...]
    all_to_all x0 -> x4, starting transfers between devices: none -> 20.4 us  [the longest x1 6.64 us: body(): lax.all_to_all(project_rows, 'tensor', split_axis=0, concat_axis=0, tiled...]
    dot_general x2, matrix products: 22.6 us -> 3.79 us  [the longest x1 1.97 us: body(): jnp.dot(own_tokens, project_rows, preferred_element_type=jnp.float32)]
    all_gather x0 -> x1, blocking collectives: none -> 18.8 us  [body(): gathered = lax.all_gather(attended, 'replica', axis=0, tiled=True)]
    all_to_all x1 -> x2, blocking collectives: 41.8 us -> 28.6 us  [the longest x1 15.9 us: body(): lax.all_to_all(placed, 'tensor', split_axis=0, concat_axis=0, tiled=True)]
  transfers between devices with their start and end apart: 2 -> 4, of which waited for: 2 -> 3; matrix products, arithmetic and copies ran while one was open for 6% -> 10% of each run, Pallas kernels for 0% -> 5%
where the time goes in v1:
time: 136 us; the launch traced here: 135 us
  blocking collectives  47.4 us (35%)
  waiting for transfers between devices  34.7 us (26%)
  starting transfers between devices  20.4 us (15%)
  matrix products  14.8 us (11%)
  Pallas kernels  10.2 us (7%)
  local copies, waits for them, and re-layouts  4.21 us (3%)
  other arithmetic  3.25 us (2%)
    all_to_all x1, waiting for transfers between devices, body(): lax.all_to_all(project_rows, 'tensor', split_axis=0, concat_axis=0, tiled...  19.6 us
    all_gather x1, blocking collectives, body(): gathered = lax.all_gather(attended, 'replica', axis=0, tiled=True)  18.8 us
    all_to_all x1, blocking collectives, body(): lax.all_to_all(placed, 'tensor', split_axis=0, concat_axis=0, tiled=True)  15.9 us
    all_to_all x1, blocking collectives, body(): lax.all_to_all(parts, 'replica', split_axis=0, concat_axis=0, tiled=True)  12.7 us
    all_to_all x1, waiting for transfers between devices, body(): lax.all_to_all(partial, 'replica', split_axis=0, concat_axis=0, tiled=True)  12.2 us
    all_to_all x1, starting transfers between devices, body(): lax.all_to_all(project_rows, 'tensor', split_axis=0, concat_axis=0, tiled...  6.64 us
    pallas_call x1, Pallas kernels, split_slices(): pl.pallas_call(slice_body, grid=(slices,), in_specs=[pl.BlockSpec((height...  6.51 us
    all_to_all x1, starting transfers between devices, body(): lax.all_to_all(token_parts, 'replica', split_axis=0, concat_axis=0, tiled...  6.51 us
  transfers between devices with their start and end apart: 4, of which 3 were waited for; matrix products, arithmetic and copies ran while one was open for 10% of the time, Pallas kernels for 5%

profile of v1, /device:TPU:0, one launch (start us, length us, event | category | flops | bytes accessed | tf_op | source)
XLA Modules:
  0.0 135.1 jit_solution(11285798812460272145)
XLA Ops:
  0.0 0.8 copy.8
  1.0 0.7 sub.40
  1.9 0.5 multiply_minimum_fusion.first_ref
  2.4 1.7 %reshape.332.tokens_ref = bf16[16,8192]{1,0:T(8,128)(2,1)} reshape(bf16[8,2,8192]{2,1,0:T(2,128)(2,1)} %param.6) | data formatting | bytes 524288 | tf_op jit(solution)/shard_map/reshape | solution.py:178
  4.2 1.7 %token_windows.1 = bf16[16,16,768]{2,1,0:T(8,128)(2,1)} custom-call(s32[16]{0:T(128)} %multiply_minimum_fusion.first_ref, bf16[16,8192]{1,0:T(8,128)(2,1)} %reshape.332.tokens_ref), custom_call_target="tpu_custom_call" | custom-call | tf_op jit(solution)/shard_map/token_windows/pallas_call | solution.py:133
  5.9 6.5 %all-to-all-start = ((bf16[16,16,768]{2,1,0:T(8,128)(2,1)}), bf16[16,16,768]{2,1,0:T(8,128)(2,1)S(1)}, u32[]{:S(2)}, u32[]{:S(2)}) async-start(bf16[16,16,768]{2,1,0:T(8,128)(2,1)} %token_windows.1), calls=%async_computation | async-start | bytes 786432 | tf_op jit(solution)/shard_map/all_to_all | solution.py:198
  12.5 6.5 %split_slices.1 = (bf16[8,72,1280]{2,1,0:T(8,128)(2,1)}, bf16[8,72,1024]{2,1,0:T(8,128)(2,1)}) custom-call(f32[68,18432]{1,0:T(8,128)} %o_ref.1, f32[68,18432]{1,0:T(8,128)} %o_ref.1, f32[68,18432]{1,0:T(8,128)} %o_ref.1, f32[68,18432]{1,0:T(8,128)} %o_ref.1), custom_call_target="tpu_custom_call" | custom-call | tf_op jit(solution)/shard_map/split_slices/pallas_call | solution.py:105
  19.0 2.9 %all-to-all-done = bf16[16,16,768]{2,1,0:T(8,128)(2,1)S(1)} async-done(((bf16[16,16,768]{2,1,0:T(8,128)(2,1)}), bf16[16,16,768]{2,1,0:T(8,128)(2,1)S(1)}, u32[]{:S(2)}, u32[]{:S(2)}) %all-to-all-start) | async-done | bytes 393248 | tf_op jit(solution)/shard_map/all_to_all | solution.py:198
  21.9 6.6 %all-to-all-start.1 = ((bf16[8,72,1280]{2,1,0:T(8,128)(2,1)}), bf16[8,72,1280]{2,1,0:T(8,128)(2,1)S(1)}, u32[]{:S(2)}, u32[]{:S(2)}) async-start(bf16[8,72,1280]{2,1,0:T(8,128)(2,1)} %get-tuple-element.7), calls=%async_computation.1 | async-start | bytes 2949120 | tf_op jit(solution)/shard_map/all_to_all | solution.py:197
  28.6 0.6 dynamic_slice.13
  29.2 0.6 subtract_select_fusion
  30.2 19.6 %all-to-all-done.1 = bf16[8,72,1280]{2,1,0:T(8,128)(2,1)S(1)} async-done(((bf16[8,72,1280]{2,1,0:T(8,128)(2,1)}), bf16[8,72,1280]{2,1,0:T(8,128)(2,1)S(1)}, u32[]{:S(2)}, u32[]{:S(2)}) %all-to-all-start.1) | async-done | bytes 1474592 | tf_op jit(solution)/shard_map/all_to_all | solution.py:197
  49.8 2.0 %convolution_convert_fusion = bf16[256,1280]{1,0:T(8,128)(2,1)} fusion(bf16[576,1280]{1,0:T(8,128)(2,1)S(1)} %bitcast.94, bf16[256,768]{1,0:T(8,128)(2,1)S(1)} %bitcast.97, s32[576]{0:T(1024)S(1)} %select_n.37), kind=kOutput, calls=%fused_computation.8 | convolution fusion | flops 604897280 | bytes 2525440 | tf_op jit(solution)/shard_map/dot_general | solution.py:206
  51.8 3.6 %all-to-all-start.2 = ((bf16[16,16,1280]{2,1,0:T(8,128)(2,1)}), bf16[16,16,1280]{2,1,0:T(8,128)(2,1)S(1)}, u32[]{:S(2)}, u32[]{:S(2)}) async-start(bf16[16,16,1280]{2,1,0:T(8,128)(2,1)} %bitcast.6), calls=%async_computation.2 | async-start | bytes 1310720 | tf_op jit(solution)/shard_map/all_to_all | solution.py:208
  55.5 12.2 %all-to-all-done.2 = bf16[16,16,1280]{2,1,0:T(8,128)(2,1)S(1)} async-done(((bf16[16,16,1280]{2,1,0:T(8,128)(2,1)}), bf16[16,16,1280]{2,1,0:T(8,128)(2,1)S(1)}, u32[]{:S(2)}, u32[]{:S(2)}) %all-to-all-start.2) | async-done | bytes 655392 | tf_op jit(solution)/shard_map/all_to_all | solution.py:208
  67.7 3.6 %all-to-all-start.3 = ((bf16[8,72,1024]{2,1,0:T(8,128)(2,1)}), bf16[8,72,1024]{2,1,0:T(8,128)(2,1)S(1)}, u32[]{:S(2)}, u32[]{:S(2)}) async-start(bf16[8,72,1024]{2,1,0:T(8,128)(2,1)} %get-tuple-element.8), calls=%async_computation.3 | async-start | bytes 2359296 | tf_op jit(solution)/shard_map/all_to_all | solution.py:199
  71.7 5.8 %fusion.48 = (f32[8,8,2]{1,2,0:T(2,128)S(1)}, f32[8,1,8,2,4096]{4,2,3,0,1:T(8,128)S(1)}) fusion(bf16[8,1,4096,128]{3,2,1,0:T(8,128)(2,1)} %param.9, bf16[8,2,8,64]{3,2,1,0:T(8,128)(2,1)S(1)} %bitcast.101, bf16[8,2,8,64]{3,2,1,0:T(8,128)(2,1)S(1)} %bitcast.99, pred[8,4096]{1,0:T(8,128)(4,1)S(1)} %iota_compare_fusion.11), kind=kOutput, calls=%fused_computation.72 | convolution fusion | flops 135856000 | bytes 10551808 | tf_op jit(solution)/shard_map/bskgd,bkcd->bkgsc/dot_general | solution.py:64
  78.4 4.7 %fusion.21 = f32[8,128,8,2]{1,2,3,0:T(8,128)S(1)} fusion(bf16[8,1,4096,128]{3,2,1,0:T(8,128)(2,1)} %param.10, f32[8,1,8,2,4096]{4,2,3,0,1:T(8,128)S(1)} %get-tuple-element.16, f32[8,8,2]{1,2,0:T(2,128)S(1)} %add.74, f32[8,8,2]{1,2,0:T(2,128)S(1)} %max.9), kind=kOutput, calls=%fused_computation.19 | convolution fusion | flops 135790592 | bytes 10552320 | tf_op jit(solution)/shard_map/bkgsc,bkcd->bskgd/dot_general | solution.py:80
  83.3 18.8 %all_gather.3 = bf16[256,1024]{1,0:T(8,128)(2,1)S(1)} all-gather(bf16[16,1024]{1,0:T(8,128)(2,1)S(1)} %bitcast.103), channel_id=1, replica_groups=mesh['replica'=16,'tensor'=8] {'replica'}, dimensions={0}, use_global_device_ids=true | all-gather | bytes 557056 | tf_op jit(solution)/shard_map/all_gather | solution.py:218
  102.1 1.8 %convolution_convert_fusion.1 = bf16[256,768]{1,0:T(8,128)(2,1)S(1)} fusion(bf16[256,1024]{1,0:T(8,128)(2,1)S(1)} %all_gather.3, bf16[576,1024]{1,0:T(8,128)(2,1)S(1)} %bitcast.95, s32[576]{0:T(1024)S(1)} %select_n.37), kind=kOutput, calls=%fused_computation.17 | convolution fusion | flops 1310048256 | bytes 2099456 | tf_op jit(solution)/shard_map/dot_general | solution.py:222
  103.9 12.7 %all_to_all.30.part_ref = bf16[16,16,768]{2,1,0:T(8,128)(2,1)} all-to-all(bf16[16,16,768]{2,1,0:T(8,128)(2,1)S(1)} %bitcast.98), channel_id=1, replica_groups=mesh['replica'=16,'tensor'=8] {'replica'}, dimensions={0} | all-to-all | bytes 786432 | tf_op jit(solution)/shard_map/all_to_all | solution.py:226
  116.6 1.9 %place_windows.1 = bf16[8,16,1024]{2,1,0:T(8,128)(2,1)} custom-call(s32[16]{0:T(128)} %multiply_minimum_fusion.first_ref, bf16[16,16,768]{2,1,0:T(8,128)(2,1)} %all_to_all.30.part_ref), custom_call_target="tpu_custom_call" | custom-call | tf_op jit(solution)/shard_map/place_windows/pallas_call | solution.py:159
  118.5 15.9 %all_to_all.31 = bf16[8,16,1024]{2,1,0:T(8,128)(2,1)S(1)} all-to-all(bf16[8,16,1024]{2,1,0:T(8,128)(2,1)} %place_windows.1), channel_id=1, replica_groups=mesh['replica'=16,'tensor'=8] {'tensor'}, dimensions={0} | all-to-all | bytes 524288 | tf_op jit(solution)/shard_map/all_to_all | solution.py:228
  134.5 0.6 reshape.347
  (35 shorter events, 2.5 us)
Async XLA Ops:
  5.9 16.0 %all-to-all-start = ((bf16[16,16,768]{2,1,0:T(8,128)(2,1)}), bf16[16,16,768]{2,1,0:T(8,128)(2,1)S(1)}, u32[]{:S(2)}, u32[]{:S(2)}) async-start(bf16[16,16,768]{2,1,0:T(8,128)(2,1)} %token_windows.1), calls=%async_computation | async-start | bytes 786432 | tf_op jit(solution)/shard_map/all_to_all | solution.py:198
  19.0 9.6 %copy-start = (s32[128]{0:T(128)S(1)}, s32[128]{0:T(128)}, u32[]{:S(2)}) copy-start(s32[128]{0:T(128)} %param.8) | copy-start | bytes 1540
  19.0 9.7 %copy-start.2 = (s32[16]{0:T(128)S(1)}, s32[16]{0:T(128)}, u32[]{:S(2)}) copy-start(s32[16]{0:T(128)} %multiply_minimum_fusion.first_ref) | copy-start | bytes 196
  19.0 11.0 %copy-start.1 = (s32[8]{0:T(128)S(1)}, s32[8]{0:T(128)}, u32[]{:S(2)}) copy-start(s32[8]{0:T(128)} %param.11) | copy-start | bytes 100
  21.9 27.9 %all-to-all-start.1 = ((bf16[8,72,1280]{2,1,0:T(8,128)(2,1)}), bf16[8,72,1280]{2,1,0:T(8,128)(2,1)S(1)}, u32[]{:S(2)}, u32[]{:S(2)}) async-start(bf16[8,72,1280]{2,1,0:T(8,128)(2,1)} %get-tuple-element.7), calls=%async_computation.1 | async-start | bytes 2949120 | tf_op jit(solution)/shard_map/all_to_all | solution.py:197
  51.8 15.9 %all-to-all-start.2 = ((bf16[16,16,1280]{2,1,0:T(8,128)(2,1)}), bf16[16,16,1280]{2,1,0:T(8,128)(2,1)S(1)}, u32[]{:S(2)}, u32[]{:S(2)}) async-start(bf16[16,16,1280]{2,1,0:T(8,128)(2,1)} %bitcast.6), calls=%async_computation.2 | async-start | bytes 1310720 | tf_op jit(solution)/shard_map/all_to_all | solution.py:208
  67.7 34.4 %all-to-all-start.3 = ((bf16[8,72,1024]{2,1,0:T(8,128)(2,1)}), bf16[8,72,1024]{2,1,0:T(8,128)(2,1)S(1)}, u32[]{:S(2)}, u32[]{:S(2)}) async-start(bf16[8,72,1024]{2,1,0:T(8,128)(2,1)} %get-tuple-element.8), calls=%async_computation.3 | async-start | bytes 2359296 | tf_op jit(solution)/shard_map/all_to_all | solution.py:199

commit v2 on v1

--- a/solution.py
+++ b/solution.py
@@ -86,41 +86,51 @@
     return mixed.astype(jnp.bfloat16).reshape(count, width_q)
 
 
-def slice_body(q_ref, k_ref, v_ref, o_ref, in_ref, out_ref):
+def project_body(q_ref, k_ref, v_ref, in_ref):
     height = q_ref.shape[0]
     qw, kw = q_ref.shape[1], k_ref.shape[1]
     in_ref[0, 0:height, 0:qw] = q_ref[...].astype(jnp.bfloat16)
     in_ref[0, 0:height, qw : qw + kw] = k_ref[...].astype(jnp.bfloat16)
     in_ref[0, 0:height, qw + kw : qw + 2 * kw] = v_ref[...].astype(jnp.bfloat16)
     in_ref[0, height:ROWS, :] = jnp.zeros((ROWS - height, qw + 2 * kw), jnp.bfloat16)
-    out_ref[0, 0:height, :] = o_ref[...].astype(jnp.bfloat16)
-    out_ref[0, height:ROWS, :] = jnp.zeros((ROWS - height, qw), jnp.bfloat16)
-
-
-def split_slices(block, slices):
+
+
+def split_project(block, slices):
     height = block.shape[0]
     qw = HQ * HD // slices
     kw = KV * HD // slices
-    project = (HQ + 2 * KV) * HD
-    return pl.pallas_call(
-        slice_body,
+    return pl.pallas_call(
+        project_body,
         grid=(slices,),
         in_specs=[
             pl.BlockSpec((height, qw), lambda t: (0, t)),
             pl.BlockSpec((height, kw), lambda t: (0, HQ * HD // kw + t)),
             pl.BlockSpec((height, kw), lambda t: (0, (HQ + KV) * HD // kw + t)),
-            pl.BlockSpec((height, qw), lambda t: (0, project // qw + t)),
         ],
-        out_specs=[
-            pl.BlockSpec((1, ROWS, qw + 2 * kw), lambda t: (t, 0, 0)),
-            pl.BlockSpec((1, ROWS, qw), lambda t: (t, 0, 0)),
-        ],
-        out_shape=[
-            jax.ShapeDtypeStruct((slices, ROWS, qw + 2 * kw), jnp.bfloat16),
-            jax.ShapeDtypeStruct((slices, ROWS, qw), jnp.bfloat16),
-        ],
-        name="split_slices",
-    )(block, block, block, block)
+        out_specs=pl.BlockSpec((1, ROWS, qw + 2 * kw), lambda t: (t, 0, 0)),
+        out_shape=jax.ShapeDtypeStruct((slices, ROWS, qw + 2 * kw), jnp.bfloat16),
+        name="split_project",
+    )(block, block, block)
+
+
+def output_body(o_ref, out_ref):
+    height, qw = o_ref.shape
+    out_ref[0, 0:height, :] = o_ref[...].astype(jnp.bfloat16)
+    out_ref[0, height:ROWS, :] = jnp.zeros((ROWS - height, qw), jnp.bfloat16)
+
+
+def split_output(block, slices):
+    height = block.shape[0]
+    qw = HQ * HD // slices
+    project = (HQ + 2 * KV) * HD
+    return pl.pallas_call(
+        output_body,
+        grid=(slices,),
+        in_specs=[pl.BlockSpec((height, qw), lambda t: (0, project // qw + t))],
+        out_specs=pl.BlockSpec((1, ROWS, qw), lambda t: (t, 0, 0)),
+        out_shape=jax.ShapeDtypeStruct((slices, ROWS, qw), jnp.bfloat16),
+        name="split_output",
+    )(block)
 
 
 def windows_body(first_ref, tokens_ref, out_ref):
@@ -169,12 +179,46 @@
     )(first, parts)
 
 
+def exchange_blocks(blocks):
+    members = blocks.shape[0]
+    mine = lax.axis_index("replica")
+    for bit in range(members.bit_length() - 1):
+        size = 1 << bit
+        low = (mine & size) == 0
+        split = blocks.reshape(members // (2 * size), 2, size, *blocks.shape[1:])
+        kept = jnp.where(low, split[:, 0], split[:, 1])
+        sent = jnp.where(low, split[:, 1], split[:, 0])
+        pairs = [(member, member ^ size) for member in range(members)]
+        got = lax.ppermute(sent, "replica", pairs)
+        blocks = jnp.stack(
+            [jnp.where(low, kept, got), jnp.where(low, got, kept)], axis=1
+        ).reshape(blocks.shape)
+    return blocks
+
+
+def gather_tokens(block):
+    replicas = lax.axis_size("replica")
+    count = block.shape[0]
+    same_core = [list(range(core, replicas, 2)) for core in range(2)]
+    other_core = [(member, member ^ 1) for member in range(replicas)]
+    mine = lax.all_gather(block, "replica", axis=0, axis_index_groups=same_core)
+    theirs = lax.ppermute(mine, "replica", other_core)
+    even = lax.axis_index("replica") % 2 == 0
+    pair = [jnp.where(even, mine, theirs), jnp.where(even, theirs, mine)]
+    return jnp.stack(pair, axis=1).reshape(replicas * count, -1)
+
+
 def body(hidden, shard_rows, piece_length, cache_keys, cache_values, cache_fill):
     slices = lax.axis_size("tensor")
     replicas = lax.axis_size("replica")
     replica = lax.axis_index("replica")
     batch_rows = cache_keys.shape[0]
     count = batch_rows * 2
+
+    project_rows, piece_length, hidden = lax.optimization_barrier(
+        (split_project(shard_rows, slices), piece_length, hidden)
+    )
+    project_rows = lax.all_to_all(project_rows, "tensor", split_axis=0, concat_axis=0, tiled=True)
     tokens = hidden.reshape(count, hidden.shape[2])
 
     piece_ends = jnp.cumsum(piece_length)
@@ -192,10 +236,10 @@
     ).reshape(-1)
     choose = (jnp.arange(WINDOW, dtype=jnp.int32)[:, None] == target[None, :]).astype(jnp.bfloat16)
 
-    project_rows, output_rows = split_slices(shard_rows, slices)
     token_parts = token_windows(tokens, first)
-    project_rows = lax.all_to_all(project_rows, "tensor", split_axis=0, concat_axis=0, tiled=True)
-    token_parts = lax.all_to_all(token_parts, "replica", split_axis=0, concat_axis=0, tiled=True)
+    token_parts, shard_rows = lax.optimization_barrier((token_parts, shard_rows))
+    token_parts = exchange_blocks(token_parts)
+    output_rows = split_output(shard_rows, slices)
     output_rows = lax.all_to_all(output_rows, "tensor", split_axis=0, concat_axis=0, tiled=True)
     project_rows = project_rows.reshape(slices * ROWS, -1)
     output_rows = output_rows.reshape(slices * ROWS, -1)
@@ -215,7 +259,7 @@
     )
     cosine, sine_part = rope_tables(position)
     attended = attend(projected, cache_keys, cache_values, cache_fill, cosine, sine_part)
-    gathered = lax.all_gather(attended, "replica", axis=0, tiled=True)
+    gathered = gather_tokens(attended)
     output_window = jnp.dot(choose, output_rows, preferred_element_type=jnp.float32).astype(
         jnp.bfloat16
     )

time: 136 us -> 148 us (1.088)
  waiting for transfers between devices: 34.7 us -> 24.7 us
  blocking collectives: 47.4 us -> 57.1 us
  starting transfers between devices: 20.4 us -> 25.9 us
  Pallas kernels: 10.2 us -> 14.8 us
  other arithmetic: 3.25 us -> 5.24 us
    all_to_all x1, waiting for transfers between devices: 19.6 us -> 0.01 us  [body(): lax.all_to_all(project_rows, 'tensor', split_axis=0, concat_axis=0, tiled...]
    ppermute x0 -> x5, waiting for transfers between devices: none -> 12.5 us  [the longest x4 10.9 us: exchange_blocks(): got = lax.ppermute(sent, 'replica', pairs)]
    all_gather x1, blocking collectives: 18.8 us -> 28.4 us  [gather_tokens(): mine = lax.all_gather(block, 'replica', axis=0, axis_index_groups=same_core)]
    ppermute x0 -> x5, starting transfers between devices: none -> 6.53 us  [the longest x4 6.53 us: exchange_blocks(): got = lax.ppermute(sent, 'replica', pairs)]
    all_to_all x1 -> x0, starting transfers between devices: 6.51 us -> none  [body(): lax.all_to_all(token_parts, 'replica', split_axis=0, concat_axis=0, tiled...]
    pallas_call x1 -> x2, Pallas kernels: 6.51 us -> 11.2 us  [the longest x1 5.68 us: split_project(): pl.pallas_call(project_body, grid=(slices,), in_specs=[pl.BlockSpec((heig...]
    all_to_all x1, starting transfers between devices: 3.63 us -> 7.8 us  [body(): lax.all_to_all(output_rows, 'tensor', split_axis=0, concat_axis=0, tiled=...]
    all_to_all x1 -> x0, waiting for transfers between devices: 2.92 us -> none  [body(): lax.all_to_all(token_parts, 'replica', split_axis=0, concat_axis=0, tiled...]
  transfers between devices with their start and end apart: 4 -> 8, of which waited for: 3 -> 4; matrix products, arithmetic and copies ran while one was open for 10% -> 13% of each run, Pallas kernels for 5% -> 5%
where the time goes in v2:
time: 148 us; the launch traced here: 147 us
  blocking collectives  57.1 us (39%)
  starting transfers between devices  25.9 us (18%)
  waiting for transfers between devices  24.7 us (17%)
  matrix products  15.3 us (10%)
  Pallas kernels  14.8 us (10%)
  other arithmetic  5.24 us (4%)
  local copies, waits for them, and re-layouts  3.38 us (2%)
    all_gather x1, blocking collectives, gather_tokens(): mine = lax.all_gather(block, 'replica', axis=0, axis_index_groups=same_core)  28.4 us
    all_to_all x1, blocking collectives, body(): lax.all_to_all(placed, 'tensor', split_axis=0, concat_axis=0, tiled=True)  16 us
    all_to_all x1, blocking collectives, body(): lax.all_to_all(parts, 'replica', split_axis=0, concat_axis=0, tiled=True)  12.7 us
    all_to_all x1, waiting for transfers between devices, body(): lax.all_to_all(partial, 'replica', split_axis=0, concat_axis=0, tiled=True)  12.2 us
    ppermute x4, waiting for transfers between devices, exchange_blocks(): got = lax.ppermute(sent, 'replica', pairs)  10.9 us
    all_to_all x1, starting transfers between devices, body(): lax.all_to_all(output_rows, 'tensor', split_axis=0, concat_axis=0, tiled=...  7.8 us
    all_to_all x1, starting transfers between devices, body(): lax.all_to_all(project_rows, 'tensor', split_axis=0, concat_axis=0, tiled...  7.15 us
    ppermute x4, starting transfers between devices, exchange_blocks(): got = lax.ppermute(sent, 'replica', pairs)  6.53 us
  transfers between devices with their start and end apart: 8, of which 4 were waited for; matrix products, arithmetic and copies ran while one was open for 13% of the time, Pallas kernels for 5%

profile of v2, /device:TPU:0, one launch (start us, length us, event | category | flops | bytes accessed | tf_op | source)
XLA Modules:
  0.0 146.7 jit_solution(2371403070813918919)
XLA Ops:
  0.0 5.7 %split_project.1 = bf16[8,72,1280]{2,1,0:T(8,128)(2,1)} custom-call(f32[68,18432]{1,0:T(8,128)} %o_ref, f32[68,18432]{1,0:T(8,128)} %o_ref, f32[68,18432]{1,0:T(8,128)} %o_ref), custom_call_target="tpu_custom_call" | custom-call | tf_op jit(solution)/shard_map/split_project/pallas_call | solution.py:102
  5.7 7.1 %all-to-all-start = ((bf16[8,72,1280]{2,1,0:T(8,128)(2,1)}), bf16[8,72,1280]{2,1,0:T(8,128)(2,1)S(1)}, u32[]{:S(2)}, u32[]{:S(2)}) async-start(bf16[8,72,1280]{2,1,0:T(8,128)(2,1)} %split_project.1), calls=%async_computation | async-start | bytes 2949120 | tf_op jit(solution)/shard_map/all_to_all | solution.py:221
  14.0 0.8 reshape.432.tokens_ref
  14.8 1.7 %token_windows.1 = bf16[16,16,768]{2,1,0:T(8,128)(2,1)} custom-call(s32[16]{0:T(128)} %multiply_minimum_fusion.first_ref, bf16[16,8192]{1,0:T(8,128)(2,1)} %reshape.432.tokens_ref), custom_call_target="tpu_custom_call" | custom-call | tf_op jit(solution)/shard_map/token_windows/pallas_call | solution.py:143
  16.5 1.0 fusion.34
  17.8 1.3 dynamic_slice.13
  19.9 1.1 broadcast_select_fusion.1
  21.1 2.0 %collective-permute-start.1 = (bf16[4,2,16,768]{3,2,0,1:T(8,128)(2,1)S(1)}, bf16[4,2,16,768]{3,2,0,1:T(8,128)(2,1)S(1)}, u32[]{:S(2)}, u32[]{:S(2)}) collective-permute-start(bf16[4,2,16,768]{3,2,0,1:T(8,128)(2,1)S(1)} %fusion.35), channel_id=1, source_target_pairs={{0,16},{8,24},{16,0},{24,8},{32,48},{40,56},{48,32},{56,40},{64,80... | collective-permute-start | bytes 589832 | tf_op jit(solution)/shard_map/ppermute | solution.py:192
  23.2 5.5 %split_output.1 = bf16[8,72,1024]{2,1,0:T(8,128)(2,1)} custom-call(f32[68,18432]{1,0:T(8,128)} %o_ref), custom_call_target="tpu_custom_call" | custom-call | tf_op jit(solution)/shard_map/split_output/pallas_call | solution.py:126
  28.8 3.7 %collective-permute-start.2 = (bf16[2,4,16,768]{3,2,0,1:T(8,128)(2,1)S(1)}, bf16[2,4,16,768]{3,2,0,1:T(8,128)(2,1)S(1)}, u32[]{:S(2)}, u32[]{:S(2)}) collective-permute-start(bf16[2,4,16,768]{3,2,0,1:T(8,128)(2,1)S(1)} %fusion.36), channel_id=1, source_target_pairs={{0,32},{8,40},{16,48},{24,56},{32,0},{40,8},{48,16},{56,24},{64,96... | collective-permute-start | bytes 589832 | tf_op jit(solution)/shard_map/ppermute | solution.py:192
  32.5 5.2 %collective-permute-done.2 = bf16[2,4,16,768]{3,2,0,1:T(8,128)(2,1)S(1)} collective-permute-done((bf16[2,4,16,768]{3,2,0,1:T(8,128)(2,1)S(1)}, bf16[2,4,16,768]{3,2,0,1:T(8,128)(2,1)S(1)}, u32[]{:S(2)}, u32[]{:S(2)}) %collective-permute-start.2) | collective-permute-done | bytes 196640 | tf_op jit(solution)/shard_map/ppermute | solution.py:192
  38.8 5.7 %collective-permute-done.3 = bf16[1,8,16,768]{3,2,1,0:T(8,128)(2,1)S(1)} collective-permute-done((bf16[1,8,16,768]{3,2,1,0:T(8,128)(2,1)S(1)}, bf16[1,8,16,768]{3,2,1,0:T(8,128)(2,1)S(1)}, u32[]{:S(2)}, u32[]{:S(2)}) %collective-permute-start.3) | collective-permute-done | bytes 196640 | tf_op jit(solution)/shard_map/ppermute | solution.py:192
  44.6 2.3 %convolution_convert_fusion = bf16[256,1280]{1,0:T(8,128)(2,1)} fusion(bf16[576,1280]{1,0:T(8,128)(2,1)S(1)} %bitcast.239, bf16[256,768]{1,0:T(8,128)(2,1)S(1)} %bitcast.243, s32[576]{0:T(1024)S(1)} %select_n.234), kind=kOutput, calls=%fused_computation.8 | convolution fusion | flops 604897280 | bytes 2525440 | tf_op jit(solution)/shard_map/dot_general | solution.py:250
  46.9 4.4 %all-to-all-start.1 = ((bf16[16,16,1280]{2,1,0:T(8,128)(2,1)}), bf16[16,16,1280]{2,1,0:T(8,128)(2,1)S(1)}, u32[]{:S(2)}, u32[]{:S(2)}) async-start(bf16[16,16,1280]{2,1,0:T(8,128)(2,1)} %bitcast.37), calls=%async_computation.1 | async-start | bytes 1310720 | tf_op jit(solution)/shard_map/all_to_all | solution.py:252
  51.4 12.2 %all-to-all-done.1 = bf16[16,16,1280]{2,1,0:T(8,128)(2,1)S(1)} async-done(((bf16[16,16,1280]{2,1,0:T(8,128)(2,1)}), bf16[16,16,1280]{2,1,0:T(8,128)(2,1)S(1)}, u32[]{:S(2)}, u32[]{:S(2)}) %all-to-all-start.1) | async-done | bytes 655392 | tf_op jit(solution)/shard_map/all_to_all | solution.py:252
  63.7 7.8 %all-to-all-start.2 = ((bf16[8,72,1024]{2,1,0:T(8,128)(2,1)}), bf16[8,72,1024]{2,1,0:T(8,128)(2,1)S(1)}, u32[]{:S(2)}, u32[]{:S(2)}) async-start(bf16[8,72,1024]{2,1,0:T(8,128)(2,1)} %split_output.1), calls=%async_computation.2 | async-start | bytes 2359296 | tf_op jit(solution)/shard_map/all_to_all | solution.py:243
  71.8 5.8 %fusion.58 = (f32[8,8,2]{1,2,0:T(2,128)S(1)}, f32[8,1,8,2,4096]{4,2,3,0,1:T(8,128)S(1)}) fusion(bf16[8,1,4096,128]{3,2,1,0:T(8,128)(2,1)} %param.9, bf16[8,2,8,64]{3,2,1,0:T(8,128)(2,1)S(1)} %bitcast.247, bf16[8,2,8,64]{3,2,1,0:T(8,128)(2,1)S(1)} %bitcast.245, pred[8,4096]{1,0:T(8,128)(4,1)S(1)} %iota_compare_fusion.11), kind=kOutput, calls=%fused_computation.106 | convolution fusion | flops 135856000 | bytes 10551808 | tf_op jit(solution)/shard_map/bskgd,bkcd->bkgsc/dot_general | solution.py:64
  78.5 4.7 %fusion.21 = f32[8,128,8,2]{1,2,3,0:T(8,128)S(1)} fusion(bf16[8,1,4096,128]{3,2,1,0:T(8,128)(2,1)} %param.10, f32[8,1,8,2,4096]{4,2,3,0,1:T(8,128)S(1)} %get-tuple-element.32, f32[8,8,2]{1,2,0:T(2,128)S(1)} %add.79, f32[8,8,2]{1,2,0:T(2,128)S(1)} %max.9), kind=kOutput, calls=%fused_computation.19 | convolution fusion | flops 135790592 | bytes 10552320 | tf_op jit(solution)/shard_map/bkgsc,bkcd->bskgd/dot_general | solution.py:80
  83.5 28.4 %all_gather.3 = bf16[8,16,1024]{2,1,0:T(8,128)(2,1)S(1)} all-gather(bf16[1,16,1024]{2,1,0:T(8,128)(2,1)S(1)} %all_gather_reshape.3), channel_id=1, replica_groups={{0,16,32,48,64,80,96,112},{8,24,40,56,72,88,104,120},{1,17,33,49,65,81,..., dimensions={0}, use_global_device_ids=true | all-gather | bytes 294912 | tf_op jit(solution)/shard_map/all_gather | solution.py:204
  111.9 1.5 %collective-permute-done.4 = bf16[8,16,1024]{2,1,0:T(8,128)(2,1)S(1)} collective-permute-done((bf16[8,16,1024]{2,1,0:T(8,128)(2,1)S(1)}, bf16[8,16,1024]{2,1,0:T(8,128)(2,1)S(1)}, u32[]{:S(2)}, u32[]{:S(2)}) %collective-permute-start.4) | collective-permute-done | bytes 262176 | tf_op jit(solution)/shard_map/ppermute | solution.py:205
  113.5 1.9 %convolution_convert_fusion.1 = bf16[256,768]{1,0:T(8,128)(2,1)S(1)} fusion(bf16[256,1024]{1,0:T(8,128)(2,1)S(1)} %bitcast.242, bf16[576,1024]{1,0:T(8,128)(2,1)S(1)} %bitcast.240, s32[576]{0:T(1024)S(1)} %select_n.234), kind=kOutput, calls=%fused_computation.17 | convolution fusion | flops 1310048256 | bytes 2099456 | tf_op jit(solution)/shard_map/dot_general | solution.py:266
  115.4 12.7 %all_to_all.25.part_ref = bf16[16,16,768]{2,1,0:T(8,128)(2,1)} all-to-all(bf16[16,16,768]{2,1,0:T(8,128)(2,1)S(1)} %bitcast.244), channel_id=1, replica_groups=mesh['replica'=16,'tensor'=8] {'replica'}, dimensions={0} | all-to-all | bytes 786432 | tf_op jit(solution)/shard_map/all_to_all | solution.py:270
  128.1 1.9 %place_windows.1 = bf16[8,16,1024]{2,1,0:T(8,128)(2,1)} custom-call(s32[16]{0:T(128)} %multiply_minimum_fusion.first_ref, bf16[16,16,768]{2,1,0:T(8,128)(2,1)} %all_to_all.25.part_ref), custom_call_target="tpu_custom_call" | custom-call | tf_op jit(solution)/shard_map/place_windows/pallas_call | solution.py:169
  130.0 16.0 %all_to_all.26 = bf16[8,16,1024]{2,1,0:T(8,128)(2,1)S(1)} all-to-all(bf16[8,16,1024]{2,1,0:T(8,128)(2,1)} %place_windows.1), channel_id=1, replica_groups=mesh['replica'=16,'tensor'=8] {'tensor'}, dimensions={0} | all-to-all | bytes 524288 | tf_op jit(solution)/shard_map/all_to_all | solution.py:272
  (57 shorter events, 5.8 us)
Async XLA Ops:
  5.7 7.2 %copy-start.1 = (s32[128]{0:T(128)S(1)}, s32[128]{0:T(128)}, u32[]{:S(2)}) copy-start(s32[128]{0:T(128)} %param.8) | copy-start | bytes 1540
  5.7 8.3 %copy-start = (bf16[8,2,8192]{2,1,0:T(2,128)(2,1)S(1)}, bf16[8,2,8192]{2,1,0:T(2,128)(2,1)}, u32[]{:S(2)}) copy-start(bf16[8,2,8192]{2,1,0:T(2,128)(2,1)} %param.6) | copy-start | bytes 786436
  5.7 38.9 %all-to-all-start = ((bf16[8,72,1280]{2,1,0:T(8,128)(2,1)}), bf16[8,72,1280]{2,1,0:T(8,128)(2,1)S(1)}, u32[]{:S(2)}, u32[]{:S(2)}) async-start(bf16[8,72,1280]{2,1,0:T(8,128)(2,1)} %split_project.1), calls=%async_computation | async-start | bytes 2949120 | tf_op jit(solution)/shard_map/all_to_all | solution.py:221
  12.8 10.2 %copy-start.2 = (s32[8]{0:T(128)S(1)}, s32[8]{0:T(128)}, u32[]{:S(2)}) copy-start(s32[8]{0:T(128)} %param.11) | copy-start | bytes 100
  17.6 2.3 %collective-permute-start = (bf16[8,1,16,768]{3,2,0,1:T(8,128)(2,1)S(1)}, bf16[8,1,16,768]{3,2,0,1:T(8,128)(2,1)S(1)}, u32[]{:S(2)}, u32[]{:S(2)}) collective-permute-start(bf16[8,1,16,768]{3,2,0,1:T(8,128)(2,1)S(1)} %fusion.34), channel_id=1, source_target_pairs={{0,8},{8,0},{16,24},{24,16},{32,40},{40,32},{48,56},{56,48},{64,72... | collective-permute-start | bytes 589832 | tf_op jit(solution)/shard_map/ppermute | solution.py:192
  21.1 7.7 %collective-permute-start.1 = (bf16[4,2,16,768]{3,2,0,1:T(8,128)(2,1)S(1)}, bf16[4,2,16,768]{3,2,0,1:T(8,128)(2,1)S(1)}, u32[]{:S(2)}, u32[]{:S(2)}) collective-permute-start(bf16[4,2,16,768]{3,2,0,1:T(8,128)(2,1)S(1)} %fusion.35), channel_id=1, source_target_pairs={{0,16},{8,24},{16,0},{24,8},{32,48},{40,56},{48,32},{56,40},{64,80... | collective-permute-start | bytes 589832 | tf_op jit(solution)/shard_map/ppermute | solution.py:192
  28.8 8.9 %collective-permute-start.2 = (bf16[2,4,16,768]{3,2,0,1:T(8,128)(2,1)S(1)}, bf16[2,4,16,768]{3,2,0,1:T(8,128)(2,1)S(1)}, u32[]{:S(2)}, u32[]{:S(2)}) collective-permute-start(bf16[2,4,16,768]{3,2,0,1:T(8,128)(2,1)S(1)} %fusion.36), channel_id=1, source_target_pairs={{0,32},{8,40},{16,48},{24,56},{32,0},{40,8},{48,16},{56,24},{64,96... | collective-permute-start | bytes 589832 | tf_op jit(solution)/shard_map/ppermute | solution.py:192
  37.9 6.6 %collective-permute-start.3 = (bf16[1,8,16,768]{3,2,1,0:T(8,128)(2,1)S(1)}, bf16[1,8,16,768]{3,2,1,0:T(8,128)(2,1)S(1)}, u32[]{:S(2)}, u32[]{:S(2)}) collective-permute-start(bf16[1,8,16,768]{3,2,1,0:T(8,128)(2,1)S(1)} %fusion.37), channel_id=1, source_target_pairs={{0,64},{8,72},{16,80},{24,88},{32,96},{40,104},{48,112},{56,120},{... | collective-permute-start | bytes 589832 | tf_op jit(solution)/shard_map/ppermute | solution.py:192
  46.9 16.7 %all-to-all-start.1 = ((bf16[16,16,1280]{2,1,0:T(8,128)(2,1)}), bf16[16,16,1280]{2,1,0:T(8,128)(2,1)S(1)}, u32[]{:S(2)}, u32[]{:S(2)}) async-start(bf16[16,16,1280]{2,1,0:T(8,128)(2,1)} %bitcast.37), calls=%async_computation.1 | async-start | bytes 1310720 | tf_op jit(solution)/shard_map/all_to_all | solution.py:252
  63.7 49.8 %all-to-all-start.2 = ((bf16[8,72,1024]{2,1,0:T(8,128)(2,1)}), bf16[8,72,1024]{2,1,0:T(8,128)(2,1)S(1)}, u32[]{:S(2)}, u32[]{:S(2)}) async-start(bf16[8,72,1024]{2,1,0:T(8,128)(2,1)} %split_output.1), calls=%async_computation.2 | async-start | bytes 2359296 | tf_op jit(solution)/shard_map/all_to_all | solution.py:243
  111.9 1.5 %collective-permute-start.4 = (bf16[8,16,1024]{2,1,0:T(8,128)(2,1)S(1)}, bf16[8,16,1024]{2,1,0:T(8,128)(2,1)S(1)}, u32[]{:S(2)}, u32[]{:S(2)}) collective-permute-start(bf16[8,16,1024]{2,1,0:T(8,128)(2,1)S(1)} %all_gather.3), channel_id=1, source_target_pairs={{0,8},{8,0},{16,24},{24,16},{32,40},{40,32},{48,56},{56,48},{64,72... | collective-permute-start | bytes 786440 | tf_op jit(solution)/shard_map/ppermute | solution.py:205

commit v3 on v2

--- a/solution.py
+++ b/solution.py
@@ -133,23 +133,59 @@
     )(block)
 
 
-def windows_body(first_ref, tokens_ref, out_ref):
-    for index in range(out_ref.shape[0]):
-        first = pl.multiple_of(first_ref[index], LANES)
-        out_ref[index] = tokens_ref[:, pl.ds(first, WINDOW)]
-
-
-def token_windows(tokens, first):
+def windows_body(first_ref, mine_ref, tokens_ref, near_ref, far_ref):
+    mine = mine_ref[0]
+    for index in range(near_ref.shape[0]):
+        near = pl.multiple_of(first_ref[mine ^ (2 * index)], LANES)
+        near_ref[index] = tokens_ref[:, pl.ds(near, WINDOW)]
+        far = pl.multiple_of(first_ref[mine ^ (2 * index + 1)], LANES)
+        far_ref[index] = tokens_ref[:, pl.ds(far, WINDOW)]
+
+
+def token_windows(tokens, first, mine):
+    shape = jax.ShapeDtypeStruct((first.shape[0] // 2, tokens.shape[0], WINDOW), tokens.dtype)
     return pl.pallas_call(
         windows_body,
         in_specs=[
             pl.BlockSpec(memory_space=pltpu.SMEM),
+            pl.BlockSpec(memory_space=pltpu.SMEM),
             pl.BlockSpec(memory_space=pltpu.VMEM),
         ],
+        out_specs=[pl.BlockSpec(memory_space=pltpu.VMEM)] * 2,
+        out_shape=[shape, shape],
+        name="token_windows",
+    )(first, mine, tokens)
+
+
+def order_body(mine_ref, *refs):
+    mine = mine_ref[0]
+    out_ref = refs[-1]
+    for index, part_ref in enumerate(refs[:-1]):
+        for core in range(2):
+            out_ref[mine ^ (2 * index + core)] = part_ref[core]
+
+
+def order_parts(parts, mine):
+    _, count, width = parts[0].shape
+    return pl.pallas_call(
+        order_body,
+        in_specs=[pl.BlockSpec(memory_space=pltpu.SMEM)]
+        + [pl.BlockSpec(memory_space=pltpu.VMEM)] * len(parts),
         out_specs=pl.BlockSpec(memory_space=pltpu.VMEM),
-        out_shape=jax.ShapeDtypeStruct((first.shape[0], tokens.shape[0], WINDOW), tokens.dtype),
-        name="token_windows",
-    )(first, tokens)
+        out_shape=jax.ShapeDtypeStruct((2 * len(parts), count, width), parts[0].dtype),
+        name="order_parts",
+    )(mine, *parts)
+
+
+def exchange_tokens(near, far, mine):
+    members = 2 * near.shape[0]
+
+    def swap(block, step):
+        return lax.ppermute(block, "replica", [(m, m ^ step) for m in range(members)])
+
+    both = jnp.stack([near, swap(far, 1)], axis=1)
+    parts = [both[0]] + [swap(both[index], 2 * index) for index in range(1, members // 2)]
+    return order_parts(parts, mine)
 
 
 def place_body(first_ref, part_ref, out_ref, acc_ref):
@@ -179,35 +215,6 @@
     )(first, parts)
 
 
-def exchange_blocks(blocks):
-    members = blocks.shape[0]
-    mine = lax.axis_index("replica")
-    for bit in range(members.bit_length() - 1):
-        size = 1 << bit
-        low = (mine & size) == 0
-        split = blocks.reshape(members // (2 * size), 2, size, *blocks.shape[1:])
-        kept = jnp.where(low, split[:, 0], split[:, 1])
-        sent = jnp.where(low, split[:, 1], split[:, 0])
-        pairs = [(member, member ^ size) for member in range(members)]
-        got = lax.ppermute(sent, "replica", pairs)
-        blocks = jnp.stack(
-            [jnp.where(low, kept, got), jnp.where(low, got, kept)], axis=1
-        ).reshape(blocks.shape)
-    return blocks
-
-
-def gather_tokens(block):
-    replicas = lax.axis_size("replica")
-    count = block.shape[0]
-    same_core = [list(range(core, replicas, 2)) for core in range(2)]
-    other_core = [(member, member ^ 1) for member in range(replicas)]
-    mine = lax.all_gather(block, "replica", axis=0, axis_index_groups=same_core)
-    theirs = lax.ppermute(mine, "replica", other_core)
-    even = lax.axis_index("replica") % 2 == 0
-    pair = [jnp.where(even, mine, theirs), jnp.where(even, theirs, mine)]
-    return jnp.stack(pair, axis=1).reshape(replicas * count, -1)
-
-
 def body(hidden, shard_rows, piece_length, cache_keys, cache_values, cache_fill):
     slices = lax.axis_size("tensor")
     replicas = lax.axis_size("replica")
@@ -236,9 +243,10 @@
     ).reshape(-1)
     choose = (jnp.arange(WINDOW, dtype=jnp.int32)[:, None] == target[None, :]).astype(jnp.bfloat16)
 
-    token_parts = token_windows(tokens, first)
-    token_parts, shard_rows = lax.optimization_barrier((token_parts, shard_rows))
-    token_parts = exchange_blocks(token_parts)
+    mine = replica.astype(jnp.int32).reshape(1)
+    near, far = token_windows(tokens, first, mine)
+    near, shard_rows = lax.optimization_barrier((near, shard_rows))
+    token_parts = exchange_tokens(near, far, mine)
     output_rows = split_output(shard_rows, slices)
     output_rows = lax.all_to_all(output_rows, "tensor", split_axis=0, concat_axis=0, tiled=True)
     project_rows = project_rows.reshape(slices * ROWS, -1)
@@ -259,7 +267,7 @@
     )
     cosine, sine_part = rope_tables(position)
     attended = attend(projected, cache_keys, cache_values, cache_fill, cosine, sine_part)
-    gathered = gather_tokens(attended)
+    gathered = lax.all_gather(attended, "replica", axis=0, tiled=True)
     output_window = jnp.dot(choose, output_rows, preferred_element_type=jnp.float32).astype(
         jnp.bfloat16
     )

time: 148 us -> 133 us (0.90)
  waiting for transfers between devices: 24.7 us -> 12.5 us
  blocking collectives: 57.1 us -> 47 us
  starting transfers between devices: 25.9 us -> 32 us
  Pallas kernels: 14.8 us -> 16.6 us
    ppermute x5 -> x8, waiting for transfers between devices: 12.5 us -> 0.3 us  [swap(): lax.ppermute(block, 'replica', [(m, m ^ step) for m in range(members)])]
    all_gather x1, blocking collectives: 28.4 us -> 18.6 us  [body(): gathered = lax.all_gather(attended, 'replica', axis=0, tiled=True)]
    ppermute x5 -> x8, starting transfers between devices: 6.53 us -> 12.7 us  [swap(): lax.ppermute(block, 'replica', [(m, m ^ step) for m in range(members)])]
    select_n x5 -> x0, other arithmetic: 2.19 us -> none  [the longest x4 1.13 us: exchange_blocks(): sent = jnp.where(low, split[:, 1], split[:, 0])]
    pallas_call x0 -> x1, Pallas kernels: none -> 1.75 us  [order_parts(): pl.pallas_call(order_body, in_specs=[pl.BlockSpec(memory_space=pltpu.SMEM...]
    squeeze x0 -> x1, other arithmetic: none -> 1.51 us  [exchange_tokens(): both[index]]
  transfers between devices with their start and end apart: 8 -> 11, of which waited for: 4 -> 2; matrix products, arithmetic and copies ran while one was open for 13% -> 13% of each run, Pallas kernels for 5% -> 7%
where the time goes in v3:
time: 133 us; the launch traced here: 132 us
  blocking collectives  47 us (35%)
  starting transfers between devices  32 us (24%)
  Pallas kernels  16.6 us (12%)
  matrix products  16 us (12%)
  waiting for transfers between devices  12.5 us (9%)
  other arithmetic  4.1 us (3%)
  local copies, waits for them, and re-layouts  3.93 us (3%)
    all_gather x1, blocking collectives, body(): gathered = lax.all_gather(attended, 'replica', axis=0, tiled=True)  18.6 us
    all_to_all x1, blocking collectives, body(): lax.all_to_all(placed, 'tensor', split_axis=0, concat_axis=0, tiled=True)  15.7 us
    all_to_all x1, blocking collectives, body(): lax.all_to_all(parts, 'replica', split_axis=0, concat_axis=0, tiled=True)  12.7 us
    ppermute x8, starting transfers between devices, swap(): lax.ppermute(block, 'replica', [(m, m ^ step) for m in range(members)])  12.7 us
    all_to_all x1, waiting for transfers between devices, body(): lax.all_to_all(partial, 'replica', split_axis=0, concat_axis=0, tiled=True)  12.2 us
    all_to_all x1, starting transfers between devices, body(): lax.all_to_all(output_rows, 'tensor', split_axis=0, concat_axis=0, tiled=...  7.81 us
    all_to_all x1, starting transfers between devices, body(): lax.all_to_all(project_rows, 'tensor', split_axis=0, concat_axis=0, tiled...  7.16 us
    dot_general x1, matrix products, attend(): jnp.einsum('bskgd,bkcd->bkgsc', query, keys_cache, preferred_element_type...  5.82 us
  transfers between devices with their start and end apart: 11, of which 2 were waited for; matrix products, arithmetic and copies ran while one was open for 13% of the time, Pallas kernels for 7%

profile of v3, /device:TPU:0, one launch (start us, length us, event | category | flops | bytes accessed | tf_op | source)
XLA Modules:
  0.0 132.4 jit_solution(4047818839341370390)
XLA Ops:
  0.0 5.7 %split_project.1 = bf16[8,72,1280]{2,1,0:T(8,128)(2,1)} custom-call(f32[68,18432]{1,0:T(8,128)} %o_ref, f32[68,18432]{1,0:T(8,128)} %o_ref, f32[68,18432]{1,0:T(8,128)} %o_ref), custom_call_target="tpu_custom_call" | custom-call | tf_op jit(solution)/shard_map/split_project/pallas_call | solution.py:102
  5.7 7.2 %all-to-all-start = ((bf16[8,72,1280]{2,1,0:T(8,128)(2,1)}), bf16[8,72,1280]{2,1,0:T(8,128)(2,1)S(1)}, u32[]{:S(2)}, u32[]{:S(2)}) async-start(bf16[8,72,1280]{2,1,0:T(8,128)(2,1)} %split_project.1), calls=%async_computation | async-start | bytes 2949120 | tf_op jit(solution)/shard_map/all_to_all | solution.py:228
  14.0 0.8 reshape.336.tokens_ref
  14.8 1.7 %token_windows.1 = (bf16[8,16,768]{2,1,0:T(8,128)(2,1)}, bf16[8,16,768]{2,1,0:T(8,128)(2,1)}) custom-call(s32[16]{0:T(128)} %multiply_minimum_fusion.first_ref, s32[1]{0:T(128)} %bitcast.1.mine_ref, bf16[16,8192]{1,0:T(8,128)(2,1)} %reshape.336.tokens_ref), custom_call_target="tpu_custom_call" | custom-call | tf_op jit(solution)/shard_map/token_windows/pallas_call | solution.py:147
  16.7 1.2 dynamic_slice.13
  18.2 1.5 %fusion.40 = (bf16[2,16,768]{2,1,0:T(8,128)(2,1)S(1)}, bf16[2,16,768]{2,1,0:T(8,128)(2,1)}, bf16[2,16,768]{2,1,0:T(8,128)(2,1)S(1)}, bf16[2,16,768]{2,1,0:T(8,12...) fusion(bf16[8,1,16,768]{3,2,1,0:T(8,128)(2,1)S(1)} %bitcast.119, ...), kind=kLoop, calls=%fused_computation.55 | loop fusion | flops 196608 | bytes 786432 | tf_op jit(solution)/shard_map/squeeze | solution.py:187
  19.7 1.9 %collective-permute-start.1 = (bf16[2,16,768]{2,1,0:T(8,128)(2,1)S(1)}, bf16[2,16,768]{2,1,0:T(8,128)(2,1)S(1)}, u32[]{:S(2)}, u32[]{:S(2)}) collective-permute-start(bf16[2,16,768]{2,1,0:T(8,128)(2,1)S(1)} %get-tuple-element.21), channel_id=1, source_target_pairs={{0,16},{8,24},{16,0},{24,8},{32,48},{40,56},{48,32},{56,40},{64,80... | collective-permute-start | bytes 147464 | tf_op jit(solution)/shard_map/ppermute | solution.py:184
  21.7 3.6 %collective-permute-start.2 = (bf16[2,16,768]{2,1,0:T(8,128)(2,1)S(1)}, bf16[2,16,768]{2,1,0:T(8,128)(2,1)S(1)}, u32[]{:S(2)}, u32[]{:S(2)}) collective-permute-start(bf16[2,16,768]{2,1,0:T(8,128)(2,1)S(1)} %get-tuple-element.22), channel_id=1, source_target_pairs={{0,32},{8,40},{16,48},{24,56},{32,0},{40,8},{48,16},{56,24},{64,96... | collective-permute-start | bytes 147464 | tf_op jit(solution)/shard_map/ppermute | solution.py:184
  25.9 0.8 collective-permute-start.4
  27.3 4.9 %collective-permute-start.6 = (bf16[2,16,768]{2,1,0:T(8,128)(2,1)S(1)}, bf16[2,16,768]{2,1,0:T(8,128)(2,1)S(1)}, u32[]{:S(2)}, u32[]{:S(2)}) collective-permute-start(bf16[2,16,768]{2,1,0:T(8,128)(2,1)S(1)} %get-tuple-element.26), channel_id=1, source_target_pairs={{0,96},{8,104},{16,112},{24,120},{32,64},{40,72},{48,80},{56,88},{... | collective-permute-start | bytes 147464 | tf_op jit(solution)/shard_map/ppermute | solution.py:184
  32.2 0.9 collective-permute-start.7
  33.1 5.5 %split_output.1 = bf16[8,72,1024]{2,1,0:T(8,128)(2,1)} custom-call(f32[68,18432]{1,0:T(8,128)} %o_ref), custom_call_target="tpu_custom_call" | custom-call | tf_op jit(solution)/shard_map/split_output/pallas_call | solution.py:126
  39.6 1.8 %order_parts.1 = bf16[16,16,768]{2,1,0:T(8,128)(2,1)} custom-call(s32[1]{0:T(128)} %bitcast.1.mine_ref, bf16[2,16,768]{2,1,0:T(8,128)(2,1)} %get-tuple-element.20.refs_0_, bf16[2,16,768]{2,1,0:T(8,128)(2,1)} %copy-done.1, bf16[2,16,768]{2,1,0:T(8,128)(2,1)} %copy-done.2, bf16[2,16,768]{2,1,0:T(8,128)(2,1)} %copy-done.3, bf16[2,16,768]{2,1,0:T(8,128)(2,1)} %copy-done.4, ...), custom_call_target="tpu_custom_call" | custom-call | tf_op jit(solution)/shard_map/order_parts/pallas_call | solution.py:170
  41.4 3.0 %convolution_convert_fusion = bf16[256,1280]{1,0:T(8,128)(2,1)} fusion(bf16[576,1280]{1,0:T(8,128)(2,1)S(1)} %bitcast.113, bf16[256,768]{1,0:T(8,128)(2,1)} %bitcast.117, s32[576]{0:T(1024)S(1)} %select_n.37), kind=kOutput, calls=%fused_computation.8 | convolution fusion | flops 604897280 | bytes 2525440 | tf_op jit(solution)/shard_map/dot_general | solution.py:258
  44.4 4.4 %all-to-all-start.1 = ((bf16[16,16,1280]{2,1,0:T(8,128)(2,1)}), bf16[16,16,1280]{2,1,0:T(8,128)(2,1)S(1)}, u32[]{:S(2)}, u32[]{:S(2)}) async-start(bf16[16,16,1280]{2,1,0:T(8,128)(2,1)} %bitcast.17), calls=%async_computation.1 | async-start | bytes 1310720 | tf_op jit(solution)/shard_map/all_to_all | solution.py:260
  48.8 12.2 %all-to-all-done.1 = bf16[16,16,1280]{2,1,0:T(8,128)(2,1)S(1)} async-done(((bf16[16,16,1280]{2,1,0:T(8,128)(2,1)}), bf16[16,16,1280]{2,1,0:T(8,128)(2,1)S(1)}, u32[]{:S(2)}, u32[]{:S(2)}) %all-to-all-start.1) | async-done | bytes 655392 | tf_op jit(solution)/shard_map/all_to_all | solution.py:260
  61.1 7.8 %all-to-all-start.2 = ((bf16[8,72,1024]{2,1,0:T(8,128)(2,1)}), bf16[8,72,1024]{2,1,0:T(8,128)(2,1)S(1)}, u32[]{:S(2)}, u32[]{:S(2)}) async-start(bf16[8,72,1024]{2,1,0:T(8,128)(2,1)} %split_output.1), calls=%async_computation.2 | async-start | bytes 2359296 | tf_op jit(solution)/shard_map/all_to_all | solution.py:251
  69.2 5.8 %fusion.63 = (f32[8,8,2]{1,2,0:T(2,128)S(1)}, f32[8,1,8,2,4096]{4,2,3,0,1:T(8,128)S(1)}) fusion(bf16[8,1,4096,128]{3,2,1,0:T(8,128)(2,1)} %param.9, bf16[8,2,8,64]{3,2,1,0:T(8,128)(2,1)S(1)} %bitcast.122, bf16[8,2,8,64]{3,2,1,0:T(8,128)(2,1)S(1)} %bitcast.120, pred[8,4096]{1,0:T(8,128)(4,1)S(1)} %iota_compare_fusion.11), kind=kOutput, calls=%fused_computation.102 | convolution fusion | flops 135856000 | bytes 10551808 | tf_op jit(solution)/shard_map/bskgd,bkcd->bkgsc/dot_general | solution.py:64
  75.9 4.7 %fusion.21 = f32[8,128,8,2]{1,2,3,0:T(8,128)S(1)} fusion(bf16[8,1,4096,128]{3,2,1,0:T(8,128)(2,1)} %param.10, f32[8,1,8,2,4096]{4,2,3,0,1:T(8,128)S(1)} %get-tuple-element.34, f32[8,8,2]{1,2,0:T(2,128)S(1)} %add.74, f32[8,8,2]{1,2,0:T(2,128)S(1)} %max.9), kind=kOutput, calls=%fused_computation.19 | convolution fusion | flops 135790592 | bytes 10552320 | tf_op jit(solution)/shard_map/bkgsc,bkcd->bskgd/dot_general | solution.py:80
  80.9 18.6 %all_gather.3 = bf16[256,1024]{1,0:T(8,128)(2,1)S(1)} all-gather(bf16[16,1024]{1,0:T(8,128)(2,1)S(1)} %bitcast.124), channel_id=1, replica_groups=mesh['replica'=16,'tensor'=8] {'replica'}, dimensions={0}, use_global_device_ids=true | all-gather | bytes 557056 | tf_op jit(solution)/shard_map/all_gather | solution.py:270
  99.5 1.9 %convolution_convert_fusion.1 = bf16[256,768]{1,0:T(8,128)(2,1)S(1)} fusion(bf16[256,1024]{1,0:T(8,128)(2,1)S(1)} %all_gather.3, bf16[576,1024]{1,0:T(8,128)(2,1)S(1)} %bitcast.114, s32[576]{0:T(1024)S(1)} %select_n.37), kind=kOutput, calls=%fused_computation.17 | convolution fusion | flops 1310048256 | bytes 2099456 | tf_op jit(solution)/shard_map/dot_general | solution.py:274
  101.4 12.7 %all_to_all.25.part_ref = bf16[16,16,768]{2,1,0:T(8,128)(2,1)} all-to-all(bf16[16,16,768]{2,1,0:T(8,128)(2,1)S(1)} %bitcast.116), channel_id=1, replica_groups=mesh['replica'=16,'tensor'=8] {'replica'}, dimensions={0} | all-to-all | bytes 786432 | tf_op jit(solution)/shard_map/all_to_all | solution.py:278
  114.1 1.9 %place_windows.1 = bf16[8,16,1024]{2,1,0:T(8,128)(2,1)} custom-call(s32[16]{0:T(128)} %multiply_minimum_fusion.first_ref, bf16[16,16,768]{2,1,0:T(8,128)(2,1)} %all_to_all.25.part_ref), custom_call_target="tpu_custom_call" | custom-call | tf_op jit(solution)/shard_map/place_windows/pallas_call | solution.py:205
  116.0 15.7 %all_to_all.26 = bf16[8,16,1024]{2,1,0:T(8,128)(2,1)S(1)} all-to-all(bf16[8,16,1024]{2,1,0:T(8,128)(2,1)} %place_windows.1), channel_id=1, replica_groups=mesh['replica'=16,'tensor'=8] {'tensor'}, dimensions={0} | all-to-all | bytes 524288 | tf_op jit(solution)/shard_map/all_to_all | solution.py:280
  (67 shorter events, 6.0 us)
Async XLA Ops:
  5.7 7.2 %copy-start.8 = (s32[128]{0:T(128)S(1)}, s32[128]{0:T(128)}, u32[]{:S(2)}) copy-start(s32[128]{0:T(128)} %param.8) | copy-start | bytes 1540
  5.7 8.3 %copy-start = (bf16[8,2,8192]{2,1,0:T(2,128)(2,1)S(1)}, bf16[8,2,8192]{2,1,0:T(2,128)(2,1)}, u32[]{:S(2)}) copy-start(bf16[8,2,8192]{2,1,0:T(2,128)(2,1)} %param.6) | copy-start | bytes 786436
  5.7 12.2 %copy-start.9 = (s32[8]{0:T(128)S(1)}, s32[8]{0:T(128)}, u32[]{:S(2)}) copy-start(s32[8]{0:T(128)} %param.11) | copy-start | bytes 100
  5.7 35.7 %all-to-all-start = ((bf16[8,72,1280]{2,1,0:T(8,128)(2,1)}), bf16[8,72,1280]{2,1,0:T(8,128)(2,1)S(1)}, u32[]{:S(2)}, u32[]{:S(2)}) async-start(bf16[8,72,1280]{2,1,0:T(8,128)(2,1)} %split_project.1), calls=%async_computation | async-start | bytes 2949120 | tf_op jit(solution)/shard_map/all_to_all | solution.py:228
  16.6 1.7 %collective-permute-start = (bf16[8,16,768]{2,1,0:T(8,128)(2,1)}, bf16[8,16,768]{2,1,0:T(8,128)(2,1)S(1)}, u32[]{:S(2)}, u32[]{:S(2)}) collective-permute-start(bf16[8,16,768]{2,1,0:T(8,128)(2,1)} %get-tuple-element.16), channel_id=1, source_target_pairs={{0,8},{8,0},{16,24},{24,16},{32,40},{40,32},{48,56},{56,48},{64,72... | collective-permute-start | bytes 589832 | tf_op jit(solution)/shard_map/ppermute | solution.py:184
  19.7 7.6 %collective-permute-start.1 = (bf16[2,16,768]{2,1,0:T(8,128)(2,1)S(1)}, bf16[2,16,768]{2,1,0:T(8,128)(2,1)S(1)}, u32[]{:S(2)}, u32[]{:S(2)}) collective-permute-start(bf16[2,16,768]{2,1,0:T(8,128)(2,1)S(1)} %get-tuple-element.21), channel_id=1, source_target_pairs={{0,16},{8,24},{16,0},{24,8},{32,48},{40,56},{48,32},{56,40},{64,80... | collective-permute-start | bytes 147464 | tf_op jit(solution)/shard_map/ppermute | solution.py:184
  21.7 10.5 %collective-permute-start.2 = (bf16[2,16,768]{2,1,0:T(8,128)(2,1)S(1)}, bf16[2,16,768]{2,1,0:T(8,128)(2,1)S(1)}, u32[]{:S(2)}, u32[]{:S(2)}) collective-permute-start(bf16[2,16,768]{2,1,0:T(8,128)(2,1)S(1)} %get-tuple-element.22), channel_id=1, source_target_pairs={{0,32},{8,40},{16,48},{24,56},{32,0},{40,8},{48,16},{56,24},{64,96... | collective-permute-start | bytes 147464 | tf_op jit(solution)/shard_map/ppermute | solution.py:184
  25.9 12.8 %collective-permute-start.3 = (bf16[2,16,768]{2,1,0:T(8,128)(2,1)S(1)}, bf16[2,16,768]{2,1,0:T(8,128)(2,1)S(1)}, u32[]{:S(2)}, u32[]{:S(2)}) collective-permute-start(bf16[2,16,768]{2,1,0:T(8,128)(2,1)S(1)} %get-tuple-element.23), channel_id=1, source_target_pairs={{0,48},{8,56},{16,32},{24,40},{32,16},{40,24},{48,0},{56,8},{64,11... | collective-permute-start | bytes 147464 | tf_op jit(solution)/shard_map/ppermute | solution.py:184
  25.9 12.7 %collective-permute-start.4 = (bf16[2,16,768]{2,1,0:T(8,128)(2,1)S(1)}, bf16[2,16,768]{2,1,0:T(8,128)(2,1)S(1)}, u32[]{:S(2)}, u32[]{:S(2)}) collective-permute-start(bf16[2,16,768]{2,1,0:T(8,128)(2,1)S(1)} %get-tuple-element.24), channel_id=1, source_target_pairs={{0,64},{8,72},{16,80},{24,88},{32,96},{40,104},{48,112},{56,120},{... | collective-permute-start | bytes 147464 | tf_op jit(solution)/shard_map/ppermute | solution.py:184
  26.7 12.0 %collective-permute-start.5 = (bf16[2,16,768]{2,1,0:T(8,128)(2,1)S(1)}, bf16[2,16,768]{2,1,0:T(8,128)(2,1)S(1)}, u32[]{:S(2)}, u32[]{:S(2)}) collective-permute-start(bf16[2,16,768]{2,1,0:T(8,128)(2,1)S(1)} %get-tuple-element.25), channel_id=1, source_target_pairs={{0,80},{8,88},{16,64},{24,72},{32,112},{40,120},{48,96},{56,104},{... | collective-permute-start | bytes 147464 | tf_op jit(solution)/shard_map/ppermute | solution.py:184
  27.3 11.3 %copy-start.1 = (bf16[2,16,768]{2,1,0:T(8,128)(2,1)}, bf16[2,16,768]{2,1,0:T(8,128)(2,1)S(1)}, u32[]{:S(2)}) copy-start(bf16[2,16,768]{2,1,0:T(8,128)(2,1)S(1)} %collective-permute-done.1.refs_1_) | copy-start | bytes 147460
  27.3 11.4 %collective-permute-start.6 = (bf16[2,16,768]{2,1,0:T(8,128)(2,1)S(1)}, bf16[2,16,768]{2,1,0:T(8,128)(2,1)S(1)}, u32[]{:S(2)}, u32[]{:S(2)}) collective-permute-start(bf16[2,16,768]{2,1,0:T(8,128)(2,1)S(1)} %get-tuple-element.26), channel_id=1, source_target_pairs={{0,96},{8,104},{16,112},{24,120},{32,64},{40,72},{48,80},{56,88},{... | collective-permute-start | bytes 147464 | tf_op jit(solution)/shard_map/ppermute | solution.py:184
  32.2 6.5 %copy-start.2 = (bf16[2,16,768]{2,1,0:T(8,128)(2,1)}, bf16[2,16,768]{2,1,0:T(8,128)(2,1)S(1)}, u32[]{:S(2)}) copy-start(bf16[2,16,768]{2,1,0:T(8,128)(2,1)S(1)} %collective-permute-done.2.refs_2_) | copy-start | bytes 147460
  32.2 6.8 %collective-permute-start.7 = (bf16[2,16,768]{2,1,0:T(8,128)(2,1)S(1)}, bf16[2,16,768]{2,1,0:T(8,128)(2,1)S(1)}, u32[]{:S(2)}, u32[]{:S(2)}) collective-permute-start(bf16[2,16,768]{2,1,0:T(8,128)(2,1)S(1)} %get-tuple-element.19), channel_id=1, source_target_pairs={{0,112},{8,120},{16,96},{24,104},{32,80},{40,88},{48,64},{56,72},{... | collective-permute-start | bytes 147464 | tf_op jit(solution)/shard_map/ppermute | solution.py:184
  38.6 0.6 copy-start.3
  38.7 0.6 copy-start.4
  38.7 0.6 copy-start.5
  38.7 0.6 copy-start.6
  39.0 0.6 copy-start.7
  44.4 16.7 %all-to-all-start.1 = ((bf16[16,16,1280]{2,1,0:T(8,128)(2,1)}), bf16[16,16,1280]{2,1,0:T(8,128)(2,1)S(1)}, u32[]{:S(2)}, u32[]{:S(2)}) async-start(bf16[16,16,1280]{2,1,0:T(8,128)(2,1)} %bitcast.17), calls=%async_computation.1 | async-start | bytes 1310720 | tf_op jit(solution)/shard_map/all_to_all | solution.py:260
  61.1 38.5 %all-to-all-start.2 = ((bf16[8,72,1024]{2,1,0:T(8,128)(2,1)}), bf16[8,72,1024]{2,1,0:T(8,128)(2,1)S(1)}, u32[]{:S(2)}, u32[]{:S(2)}) async-start(bf16[8,72,1024]{2,1,0:T(8,128)(2,1)} %split_output.1), calls=%async_computation.2 | async-start | bytes 2359296 | tf_op jit(solution)/shard_map/all_to_all | solution.py:251

commit v4 on v3

--- a/solution.py
+++ b/solution.py
@@ -188,31 +188,34 @@
     return order_parts(parts, mine)
 
 
-def place_body(first_ref, part_ref, out_ref, acc_ref):
+def place_body(first_ref, mine_ref, part_ref, *refs):
+    out_refs, acc_ref = refs[:-1], refs[-1]
     acc_ref[...] = jnp.zeros_like(acc_ref)
     for index in range(part_ref.shape[0]):
         first = pl.multiple_of(first_ref[index], LANES)
         acc_ref[:, pl.ds(first, WINDOW)] = acc_ref[:, pl.ds(first, WINDOW)] + part_ref[
             index
         ].astype(jnp.float32)
-    width = out_ref.shape[2]
-    for index in range(out_ref.shape[0]):
-        out_ref[index] = acc_ref[:, index * width : (index + 1) * width].astype(out_ref.dtype)
-
-
-def place_windows(parts, first, slices):
+    width = out_refs[0].shape[1]
+    for index, out_ref in enumerate(out_refs):
+        column = pl.multiple_of((mine_ref[0] ^ index) * width, LANES)
+        out_ref[...] = acc_ref[:, pl.ds(column, width)].astype(out_ref.dtype)
+
+
+def place_windows(parts, first, mine, slices):
     count = parts.shape[1]
     return pl.pallas_call(
         place_body,
         in_specs=[
             pl.BlockSpec(memory_space=pltpu.SMEM),
+            pl.BlockSpec(memory_space=pltpu.SMEM),
             pl.BlockSpec(memory_space=pltpu.VMEM),
         ],
-        out_specs=pl.BlockSpec(memory_space=pltpu.VMEM),
-        out_shape=jax.ShapeDtypeStruct((slices, count, D // slices), parts.dtype),
+        out_specs=[pl.BlockSpec(memory_space=pltpu.VMEM)] * slices,
+        out_shape=[jax.ShapeDtypeStruct((count, D // slices), parts.dtype)] * slices,
         scratch_shapes=[pltpu.VMEM((count, D), jnp.float32)],
         name="place_windows",
-    )(first, parts)
+    )(first, mine, parts)
 
 
 def body(hidden, shard_rows, piece_length, cache_keys, cache_values, cache_fill):
@@ -245,19 +248,19 @@
 
     mine = replica.astype(jnp.int32).reshape(1)
     near, far = token_windows(tokens, first, mine)
-    near, shard_rows = lax.optimization_barrier((near, shard_rows))
     token_parts = exchange_tokens(near, far, mine)
-    output_rows = split_output(shard_rows, slices)
-    output_rows = lax.all_to_all(output_rows, "tensor", split_axis=0, concat_axis=0, tiled=True)
     project_rows = project_rows.reshape(slices * ROWS, -1)
-    output_rows = output_rows.reshape(slices * ROWS, -1)
 
     own_tokens = jnp.dot(
         token_parts.reshape(replicas * count, WINDOW), choose, preferred_element_type=jnp.float32
     ).astype(jnp.bfloat16)
     partial = jnp.dot(own_tokens, project_rows, preferred_element_type=jnp.float32)
     partial = partial.astype(jnp.bfloat16).reshape(replicas, count, -1)
+    partial, shard_rows = lax.optimization_barrier((partial, shard_rows))
+    output_rows = split_output(shard_rows, slices)
     partial = lax.all_to_all(partial, "replica", split_axis=0, concat_axis=0, tiled=True)
+    output_rows = lax.all_to_all(output_rows, "tensor", split_axis=0, concat_axis=0, tiled=True)
+    output_rows = output_rows.reshape(slices * ROWS, -1)
     projected = jnp.sum(partial.astype(jnp.float32), axis=0)
 
     position = (
@@ -276,9 +279,13 @@
     )
     parts = parts.astype(jnp.bfloat16).reshape(replicas, count, WINDOW)
     parts = lax.all_to_all(parts, "replica", split_axis=0, concat_axis=0, tiled=True)
-    placed = place_windows(parts, first, slices)
-    placed = lax.all_to_all(placed, "tensor", split_axis=0, concat_axis=0, tiled=True)
-    result = jnp.sum(placed.astype(jnp.float32), axis=0).astype(jnp.bfloat16)
+    own_slice = lax.axis_index("tensor").astype(jnp.int32).reshape(1)
+    placed = place_windows(parts, first, own_slice, slices)
+    placed = [placed[0]] + [
+        lax.ppermute(placed[step], "tensor", [(m, m ^ step) for m in range(slices)])
+        for step in range(1, slices)
+    ]
+    result = sum(block.astype(jnp.float32) for block in placed).astype(jnp.bfloat16)
     return result.reshape(batch_rows, 2, -1)
 
 

time: 133 us -> 137 us (1.030)
  blocking collectives: 47 us -> 18.7 us
  starting transfers between devices: 32 us -> 47.1 us
  waiting for transfers between devices: 12.5 us -> 26.3 us
    all_to_all x2 -> x0, blocking collectives: 28.5 us -> none  [the longest x1 15.7 us: body(): lax.all_to_all(placed, 'tensor', split_axis=0, concat_axis=0, tiled=True)]
    ppermute x0 -> x7, starting transfers between devices: none -> 13 us  [body(): lax.ppermute(placed[step], 'tensor', [(m, m ^ step) for m in range(slices)])]
    all_to_all x0 -> x1, waiting for transfers between devices: none -> 9.41 us  [body(): lax.all_to_all(parts, 'replica', split_axis=0, concat_axis=0, tiled=True)]
    all_to_all x1, waiting for transfers between devices: 12.2 us -> 6.69 us  [body(): lax.all_to_all(partial, 'replica', split_axis=0, concat_axis=0, tiled=True)]
    ppermute x8, waiting for transfers between devices: 0.3 us -> 5.83 us  [swap(): lax.ppermute(block, 'replica', [(m, m ^ step) for m in range(members)])]
    ppermute x0 -> x7, waiting for transfers between devices: none -> 4.41 us  [body(): lax.ppermute(placed[step], 'tensor', [(m, m ^ step) for m in range(slices)])]
    all_to_all x0 -> x1, starting transfers between devices: none -> 3.55 us  [body(): lax.all_to_all(parts, 'replica', split_axis=0, concat_axis=0, tiled=True)]
  transfers between devices with their start and end apart: 11 -> 19, of which waited for: 2 -> 10; matrix products, arithmetic and copies ran while one was open for 13% -> 13% of each run, Pallas kernels for 7% -> 7%
where the time goes in v4:
time: 137 us; the launch traced here: 135 us
  starting transfers between devices  47.1 us (34%)
  waiting for transfers between devices  26.3 us (19%)
  blocking collectives  18.7 us (14%)
  matrix products  16.6 us (12%)
  Pallas kernels  16.5 us (12%)
  other arithmetic  5.01 us (4%)
  local copies, waits for them, and re-layouts  4.74 us (3%)
    all_gather x1, blocking collectives, body(): gathered = lax.all_gather(attended, 'replica', axis=0, tiled=True)  18.7 us
    ppermute x7, starting transfers between devices, body(): lax.ppermute(placed[step], 'tensor', [(m, m ^ step) for m in range(slices)])  13 us
    ppermute x8, starting transfers between devices, swap(): lax.ppermute(block, 'replica', [(m, m ^ step) for m in range(members)])  12.7 us
    all_to_all x1, waiting for transfers between devices, body(): lax.all_to_all(parts, 'replica', split_axis=0, concat_axis=0, tiled=True)  9.41 us
    all_to_all x1, starting transfers between devices, body(): lax.all_to_all(output_rows, 'tensor', split_axis=0, concat_axis=0, tiled=...  7.2 us
    all_to_all x1, starting transfers between devices, body(): lax.all_to_all(project_rows, 'tensor', split_axis=0, concat_axis=0, tiled...  7.16 us
    all_to_all x1, waiting for transfers between devices, body(): lax.all_to_all(partial, 'replica', split_axis=0, concat_axis=0, tiled=True)  6.69 us
    ppermute x8, waiting for transfers between devices, swap(): lax.ppermute(block, 'replica', [(m, m ^ step) for m in range(members)])  5.83 us
  transfers between devices with their start and end apart: 19, of which 10 were waited for; matrix products, arithmetic and copies ran while one was open for 13% of the time, Pallas kernels for 7%

profile of v4, /device:TPU:0, one launch (start us, length us, event | category | flops | bytes accessed | tf_op | source)
XLA Modules:
  0.0 135.3 jit_solution(17630067655397250292)
XLA Ops:
  0.0 5.7 %split_project.1 = bf16[8,72,1280]{2,1,0:T(8,128)(2,1)} custom-call(f32[68,18432]{1,0:T(8,128)} %o_ref, f32[68,18432]{1,0:T(8,128)} %o_ref, f32[68,18432]{1,0:T(8,128)} %o_ref), custom_call_target="tpu_custom_call" | custom-call | tf_op jit(solution)/shard_map/split_project/pallas_call | solution.py:102
  5.7 7.2 %all-to-all-start = ((bf16[8,72,1280]{2,1,0:T(8,128)(2,1)}), bf16[8,72,1280]{2,1,0:T(8,128)(2,1)S(1)}, u32[]{:S(2)}, u32[]{:S(2)}) async-start(bf16[8,72,1280]{2,1,0:T(8,128)(2,1)} %split_project.1), calls=%async_computation | async-start | bytes 2949120 | tf_op jit(solution)/shard_map/all_to_all | solution.py:231
  14.9 1.7 %token_windows.1 = (bf16[8,16,768]{2,1,0:T(8,128)(2,1)}, bf16[8,16,768]{2,1,0:T(8,128)(2,1)}) custom-call(s32[16]{0:T(128)} %multiply_minimum_fusion.first_ref, s32[1]{0:T(128)} %bitcast.2.mine_ref, bf16[16,8192]{1,0:T(8,128)(2,1)} %reshape.340.tokens_ref), custom_call_target="tpu_custom_call" | custom-call | tf_op jit(solution)/shard_map/token_windows/pallas_call | solution.py:147
  19.9 1.9 %collective-permute-start.1 = (bf16[2,16,768]{2,1,0:T(8,128)(2,1)S(1)}, bf16[2,16,768]{2,1,0:T(8,128)(2,1)S(1)}, u32[]{:S(2)}, u32[]{:S(2)}) collective-permute-start(bf16[2,16,768]{2,1,0:T(8,128)(2,1)S(1)} %get-tuple-element.37), channel_id=1, source_target_pairs={{0,16},{8,24},{16,0},{24,8},{32,48},{40,56},{48,32},{56,40},{64,80... | collective-permute-start | bytes 147464 | tf_op jit(solution)/shard_map/ppermute | solution.py:184
  21.8 3.6 %collective-permute-start.2 = (bf16[2,16,768]{2,1,0:T(8,128)(2,1)S(1)}, bf16[2,16,768]{2,1,0:T(8,128)(2,1)S(1)}, u32[]{:S(2)}, u32[]{:S(2)}) collective-permute-start(bf16[2,16,768]{2,1,0:T(8,128)(2,1)S(1)} %get-tuple-element.38), channel_id=1, source_target_pairs={{0,32},{8,40},{16,48},{24,56},{32,0},{40,8},{48,16},{56,24},{64,96... | collective-permute-start | bytes 147464 | tf_op jit(solution)/shard_map/ppermute | solution.py:184
  27.5 4.9 %collective-permute-start.6 = (bf16[2,16,768]{2,1,0:T(8,128)(2,1)S(1)}, bf16[2,16,768]{2,1,0:T(8,128)(2,1)S(1)}, u32[]{:S(2)}, u32[]{:S(2)}) collective-permute-start(bf16[2,16,768]{2,1,0:T(8,128)(2,1)S(1)} %get-tuple-element.42), channel_id=1, source_target_pairs={{0,96},{8,104},{16,112},{24,120},{32,64},{40,72},{48,80},{56,88},{... | collective-permute-start | bytes 147464 | tf_op jit(solution)/shard_map/ppermute | solution.py:184
  34.8 3.2 %collective-permute-done.6.refs_6_ = bf16[2,16,768]{2,1,0:T(8,128)(2,1)S(1)} collective-permute-done((bf16[2,16,768]{2,1,0:T(8,128)(2,1)S(1)}, bf16[2,16,768]{2,1,0:T(8,128)(2,1)S(1)}, u32[]{:S(2)}, u32[]{:S(2)}) %collective-permute-start.6) | collective-permute-done | bytes 49184 | tf_op jit(solution)/shard_map/ppermute | solution.py:184
  39.8 1.7 %order_parts.1 = bf16[16,16,768]{2,1,0:T(8,128)(2,1)} custom-call(s32[1]{0:T(128)} %bitcast.2.mine_ref, bf16[2,16,768]{2,1,0:T(8,128)(2,1)} %get-tuple-element.36.refs_0_, bf16[2,16,768]{2,1,0:T(8,128)(2,1)} %copy-done.2, bf16[2,16,768]{2,1,0:T(8,128)(2,1)} %copy-done.3, bf16[2,16,768]{2,1,0:T(8,128)(2,1)} %copy-done.4, bf16[2,16,768]{2,1,0:T(8,128)(2,1)} %copy-done.5, ...), custom_call_target="tpu_custom_call" | custom-call | tf_op jit(solution)/shard_map/order_parts/pallas_call | solution.py:170
  41.6 3.0 %convolution_convert_fusion = bf16[256,1280]{1,0:T(8,128)(2,1)} fusion(bf16[576,1280]{1,0:T(8,128)(2,1)S(1)} %bitcast.114, bf16[256,768]{1,0:T(8,128)(2,1)} %bitcast.117, s32[576]{0:T(1024)S(1)} %select_n.37), kind=kOutput, calls=%fused_computation.8 | convolution fusion | flops 604897280 | bytes 2525440 | tf_op jit(solution)/shard_map/dot_general | solution.py:257
  44.6 3.6 %all-to-all-start.1 = ((bf16[16,16,1280]{2,1,0:T(8,128)(2,1)}), bf16[16,16,1280]{2,1,0:T(8,128)(2,1)S(1)}, u32[]{:S(2)}, u32[]{:S(2)}) async-start(bf16[16,16,1280]{2,1,0:T(8,128)(2,1)} %bitcast.18), calls=%async_computation.1 | async-start | bytes 1310720 | tf_op jit(solution)/shard_map/all_to_all | solution.py:261
  48.2 5.5 %split_output.1 = bf16[8,72,1024]{2,1,0:T(8,128)(2,1)} custom-call(f32[68,18432]{1,0:T(8,128)} %o_ref), custom_call_target="tpu_custom_call" | custom-call | tf_op jit(solution)/shard_map/split_output/pallas_call | solution.py:126
  53.7 6.7 %all-to-all-done.1 = bf16[16,16,1280]{2,1,0:T(8,128)(2,1)S(1)} async-done(((bf16[16,16,1280]{2,1,0:T(8,128)(2,1)}), bf16[16,16,1280]{2,1,0:T(8,128)(2,1)S(1)}, u32[]{:S(2)}, u32[]{:S(2)}) %all-to-all-start.1) | async-done | bytes 655392 | tf_op jit(solution)/shard_map/all_to_all | solution.py:261
  60.4 7.2 %all-to-all-start.2 = ((bf16[8,72,1024]{2,1,0:T(8,128)(2,1)}), bf16[8,72,1024]{2,1,0:T(8,128)(2,1)S(1)}, u32[]{:S(2)}, u32[]{:S(2)}) async-start(bf16[8,72,1024]{2,1,0:T(8,128)(2,1)} %split_output.1), calls=%async_computation.2 | async-start | bytes 2359296 | tf_op jit(solution)/shard_map/all_to_all | solution.py:262
  68.0 5.8 %fusion.63 = (f32[8,8,2]{1,2,0:T(2,128)S(1)}, f32[8,1,8,2,4096]{4,2,3,0,1:T(8,128)S(1)}) fusion(bf16[8,1,4096,128]{3,2,1,0:T(8,128)(2,1)} %param.9, bf16[8,2,8,64]{3,2,1,0:T(8,128)(2,1)S(1)} %bitcast.122, bf16[8,2,8,64]{3,2,1,0:T(8,128)(2,1)S(1)} %bitcast.120, pred[8,4096]{1,0:T(8,128)(4,1)S(1)} %iota_compare_fusion.11), kind=kOutput, calls=%fused_computation.103 | convolution fusion | flops 135856000 | bytes 10551808 | tf_op jit(solution)/shard_map/bskgd,bkcd->bkgsc/dot_general | solution.py:64
  74.7 4.7 %fusion.21 = f32[8,128,8,2]{1,2,3,0:T(8,128)S(1)} fusion(bf16[8,1,4096,128]{3,2,1,0:T(8,128)(2,1)} %param.10, f32[8,1,8,2,4096]{4,2,3,0,1:T(8,128)S(1)} %get-tuple-element.50, f32[8,8,2]{1,2,0:T(2,128)S(1)} %add.95, f32[8,8,2]{1,2,0:T(2,128)S(1)} %max.9), kind=kOutput, calls=%fused_computation.19 | convolution fusion | flops 135790592 | bytes 10552320 | tf_op jit(solution)/shard_map/bkgsc,bkcd->bskgd/dot_general | solution.py:80
  79.6 18.7 %all_gather.3 = bf16[256,1024]{1,0:T(8,128)(2,1)S(1)} all-gather(bf16[16,1024]{1,0:T(8,128)(2,1)S(1)} %bitcast.124), channel_id=1, replica_groups=mesh['replica'=16,'tensor'=8] {'replica'}, dimensions={0}, use_global_device_ids=true | all-gather | bytes 557056 | tf_op jit(solution)/shard_map/all_gather | solution.py:273
  98.3 2.6 %convolution_convert_fusion.1 = bf16[256,768]{1,0:T(8,128)(2,1)} fusion(bf16[256,1024]{1,0:T(8,128)(2,1)S(1)} %all_gather.3, bf16[576,1024]{1,0:T(8,128)(2,1)S(1)} %bitcast.115, s32[576]{0:T(1024)S(1)} %select_n.37), kind=kOutput, calls=%fused_computation.17 | convolution fusion | flops 1310048256 | bytes 2099456 | tf_op jit(solution)/shard_map/dot_general | solution.py:277
  100.9 3.6 %all-to-all-start.3 = ((bf16[16,16,768]{2,1,0:T(8,128)(2,1)}), bf16[16,16,768]{2,1,0:T(8,128)(2,1)S(1)}, u32[]{:S(2)}, u32[]{:S(2)}) async-start(bf16[16,16,768]{2,1,0:T(8,128)(2,1)} %bitcast.46), calls=%async_computation.3 | async-start | bytes 786432 | tf_op jit(solution)/shard_map/all_to_all | solution.py:281
  104.4 9.4 %all-to-all-done.3.part_ref = bf16[16,16,768]{2,1,0:T(8,128)(2,1)S(1)} async-done(((bf16[16,16,768]{2,1,0:T(8,128)(2,1)}), bf16[16,16,768]{2,1,0:T(8,128)(2,1)S(1)}, u32[]{:S(2)}, u32[]{:S(2)}) %all-to-all-start.3) | async-done | bytes 393248 | tf_op jit(solution)/shard_map/all_to_all | solution.py:281
  114.6 1.9 %place_windows.1 = (bf16[16,1024]{1,0:T(8,128)(2,1)}, bf16[16,1024]{1,0:T(8,128)(2,1)}, bf16[16,1024]{1,0:T(8,128)(2,1)}, bf16[16,1024]{1,0:T(8,128)(2,1)}, bf16...) custom-call(s32[16]{0:T(128)} %multiply_minimum_fusion.first_ref, ...), custom_call_target="tpu_custom_call" | custom-call | tf_op jit(solution)/shard_map/place_windows/pallas_call | solution.py:207
  116.5 5.2 %collective-permute-start.14 = (bf16[16,1024]{1,0:T(8,128)(2,1)}, bf16[16,1024]{1,0:T(8,128)(2,1)S(1)}, u32[]{:S(2)}, u32[]{:S(2)}) collective-permute-start(bf16[16,1024]{1,0:T(8,128)(2,1)} %get-tuple-element.34), channel_id=1, source_target_pairs={{0,7},{1,6},{2,5},{3,4},{4,3},{5,2},{6,1},{7,0},{8,15},{9,14},{10,... | collective-permute-start | bytes 98312 | tf_op jit(solution)/shard_map/ppermute | solution.py:285
  122.1 3.5 %collective-permute-start.12 = (bf16[16,1024]{1,0:T(8,128)(2,1)}, bf16[16,1024]{1,0:T(8,128)(2,1)S(1)}, u32[]{:S(2)}, u32[]{:S(2)}) collective-permute-start(bf16[16,1024]{1,0:T(8,128)(2,1)} %get-tuple-element.32), channel_id=1, source_target_pairs={{0,5},{1,4},{2,7},{3,6},{4,1},{5,0},{6,3},{7,2},{8,13},{9,12},{10,... | collective-permute-start | bytes 98312 | tf_op jit(solution)/shard_map/ppermute | solution.py:285
  126.0 2.2 %collective-permute-start.10 = (bf16[16,1024]{1,0:T(8,128)(2,1)}, bf16[16,1024]{1,0:T(8,128)(2,1)S(1)}, u32[]{:S(2)}, u32[]{:S(2)}) collective-permute-start(bf16[16,1024]{1,0:T(8,128)(2,1)} %get-tuple-element.30), channel_id=1, source_target_pairs={{0,3},{1,2},{2,1},{3,0},{4,7},{5,6},{6,5},{7,4},{8,11},{9,10},{10,... | collective-permute-start | bytes 98312 | tf_op jit(solution)/shard_map/ppermute | solution.py:285
  131.4 2.4 %collective-permute-done.9 = bf16[16,1024]{1,0:T(8,128)(2,1)S(1)} collective-permute-done((bf16[16,1024]{1,0:T(8,128)(2,1)}, bf16[16,1024]{1,0:T(8,128)(2,1)S(1)}, u32[]{:S(2)}, u32[]{:S(2)}) %collective-permute-start.9) | collective-permute-done | bytes 32800 | tf_op jit(solution)/shard_map/ppermute | solution.py:285
  (83 shorter events, 19.3 us)
Async XLA Ops:
  5.7 7.2 %copy-start.9 = (s32[128]{0:T(128)S(1)}, s32[128]{0:T(128)}, u32[]{:S(2)}) copy-start(s32[128]{0:T(128)} %param.8) | copy-start | bytes 1540
  5.7 8.4 %copy-start.1 = (bf16[8,2,8192]{2,1,0:T(2,128)(2,1)S(1)}, bf16[8,2,8192]{2,1,0:T(2,128)(2,1)}, u32[]{:S(2)}) copy-start(bf16[8,2,8192]{2,1,0:T(2,128)(2,1)} %param.6) | copy-start | bytes 786436
  5.7 12.4 %copy-start.10 = (s32[8]{0:T(128)S(1)}, s32[8]{0:T(128)}, u32[]{:S(2)}) copy-start(s32[8]{0:T(128)} %param.11) | copy-start | bytes 100
  5.7 35.9 %all-to-all-start = ((bf16[8,72,1280]{2,1,0:T(8,128)(2,1)}), bf16[8,72,1280]{2,1,0:T(8,128)(2,1)S(1)}, u32[]{:S(2)}, u32[]{:S(2)}) async-start(bf16[8,72,1280]{2,1,0:T(8,128)(2,1)} %split_project.1), calls=%async_computation | async-start | bytes 2949120 | tf_op jit(solution)/shard_map/all_to_all | solution.py:231
  16.6 1.7 %collective-permute-start = (bf16[8,16,768]{2,1,0:T(8,128)(2,1)}, bf16[8,16,768]{2,1,0:T(8,128)(2,1)S(1)}, u32[]{:S(2)}, u32[]{:S(2)}) collective-permute-start(bf16[8,16,768]{2,1,0:T(8,128)(2,1)} %get-tuple-element.23), channel_id=1, source_target_pairs={{0,8},{8,0},{16,24},{24,16},{32,40},{40,32},{48,56},{56,48},{64,72... | collective-permute-start | bytes 589832 | tf_op jit(solution)/shard_map/ppermute | solution.py:184
  19.9 7.7 %collective-permute-start.1 = (bf16[2,16,768]{2,1,0:T(8,128)(2,1)S(1)}, bf16[2,16,768]{2,1,0:T(8,128)(2,1)S(1)}, u32[]{:S(2)}, u32[]{:S(2)}) collective-permute-start(bf16[2,16,768]{2,1,0:T(8,128)(2,1)S(1)} %get-tuple-element.37), channel_id=1, source_target_pairs={{0,16},{8,24},{16,0},{24,8},{32,48},{40,56},{48,32},{56,40},{64,80... | collective-permute-start | bytes 147464 | tf_op jit(solution)/shard_map/ppermute | solution.py:184
  21.8 10.6 %collective-permute-start.2 = (bf16[2,16,768]{2,1,0:T(8,128)(2,1)S(1)}, bf16[2,16,768]{2,1,0:T(8,128)(2,1)S(1)}, u32[]{:S(2)}, u32[]{:S(2)}) collective-permute-start(bf16[2,16,768]{2,1,0:T(8,128)(2,1)S(1)} %get-tuple-element.38), channel_id=1, source_target_pairs={{0,32},{8,40},{16,48},{24,56},{32,0},{40,8},{48,16},{56,24},{64,96... | collective-permute-start | bytes 147464 | tf_op jit(solution)/shard_map/ppermute | solution.py:184
  26.1 7.3 %collective-permute-start.3 = (bf16[2,16,768]{2,1,0:T(8,128)(2,1)S(1)}, bf16[2,16,768]{2,1,0:T(8,128)(2,1)S(1)}, u32[]{:S(2)}, u32[]{:S(2)}) collective-permute-start(bf16[2,16,768]{2,1,0:T(8,128)(2,1)S(1)} %get-tuple-element.39), channel_id=1, source_target_pairs={{0,48},{8,56},{16,32},{24,40},{32,16},{40,24},{48,0},{56,8},{64,11... | collective-permute-start | bytes 147464 | tf_op jit(solution)/shard_map/ppermute | solution.py:184
  26.1 7.3 %collective-permute-start.4 = (bf16[2,16,768]{2,1,0:T(8,128)(2,1)S(1)}, bf16[2,16,768]{2,1,0:T(8,128)(2,1)S(1)}, u32[]{:S(2)}, u32[]{:S(2)}) collective-permute-start(bf16[2,16,768]{2,1,0:T(8,128)(2,1)S(1)} %get-tuple-element.40), channel_id=1, source_target_pairs={{0,64},{8,72},{16,80},{24,88},{32,96},{40,104},{48,112},{56,120},{... | collective-permute-start | bytes 147464 | tf_op jit(solution)/shard_map/ppermute | solution.py:184
  26.9 7.9 %collective-permute-start.5 = (bf16[2,16,768]{2,1,0:T(8,128)(2,1)S(1)}, bf16[2,16,768]{2,1,0:T(8,128)(2,1)S(1)}, u32[]{:S(2)}, u32[]{:S(2)}) collective-permute-start(bf16[2,16,768]{2,1,0:T(8,128)(2,1)S(1)} %get-tuple-element.41), channel_id=1, source_target_pairs={{0,80},{8,88},{16,64},{24,72},{32,112},{40,120},{48,96},{56,104},{... | collective-permute-start | bytes 147464 | tf_op jit(solution)/shard_map/ppermute | solution.py:184
  27.5 11.7 %copy-start.2 = (bf16[2,16,768]{2,1,0:T(8,128)(2,1)}, bf16[2,16,768]{2,1,0:T(8,128)(2,1)S(1)}, u32[]{:S(2)}) copy-start(bf16[2,16,768]{2,1,0:T(8,128)(2,1)S(1)} %collective-permute-done.1.refs_1_) | copy-start | bytes 147460
  27.5 10.5 %collective-permute-start.6 = (bf16[2,16,768]{2,1,0:T(8,128)(2,1)S(1)}, bf16[2,16,768]{2,1,0:T(8,128)(2,1)S(1)}, u32[]{:S(2)}, u32[]{:S(2)}) collective-permute-start(bf16[2,16,768]{2,1,0:T(8,128)(2,1)S(1)} %get-tuple-element.42), channel_id=1, source_target_pairs={{0,96},{8,104},{16,112},{24,120},{32,64},{40,72},{48,80},{56,88},{... | collective-permute-start | bytes 147464 | tf_op jit(solution)/shard_map/ppermute | solution.py:184
  32.4 6.8 %copy-start.3 = (bf16[2,16,768]{2,1,0:T(8,128)(2,1)}, bf16[2,16,768]{2,1,0:T(8,128)(2,1)S(1)}, u32[]{:S(2)}) copy-start(bf16[2,16,768]{2,1,0:T(8,128)(2,1)S(1)} %collective-permute-done.2.refs_2_) | copy-start | bytes 147460
  32.4 6.8 %collective-permute-start.7 = (bf16[2,16,768]{2,1,0:T(8,128)(2,1)S(1)}, bf16[2,16,768]{2,1,0:T(8,128)(2,1)S(1)}, u32[]{:S(2)}, u32[]{:S(2)}) collective-permute-start(bf16[2,16,768]{2,1,0:T(8,128)(2,1)S(1)} %get-tuple-element.35), channel_id=1, source_target_pairs={{0,112},{8,120},{16,96},{24,104},{32,80},{40,88},{48,64},{56,72},{... | collective-permute-start | bytes 147464 | tf_op jit(solution)/shard_map/ppermute | solution.py:184
  44.6 15.9 %all-to-all-start.1 = ((bf16[16,16,1280]{2,1,0:T(8,128)(2,1)}), bf16[16,16,1280]{2,1,0:T(8,128)(2,1)S(1)}, u32[]{:S(2)}, u32[]{:S(2)}) async-start(bf16[16,16,1280]{2,1,0:T(8,128)(2,1)} %bitcast.18), calls=%async_computation.1 | async-start | bytes 1310720 | tf_op jit(solution)/shard_map/all_to_all | solution.py:261
  60.4 37.9 %all-to-all-start.2 = ((bf16[8,72,1024]{2,1,0:T(8,128)(2,1)}), bf16[8,72,1024]{2,1,0:T(8,128)(2,1)S(1)}, u32[]{:S(2)}, u32[]{:S(2)}) async-start(bf16[8,72,1024]{2,1,0:T(8,128)(2,1)} %split_output.1), calls=%async_computation.2 | async-start | bytes 2359296 | tf_op jit(solution)/shard_map/all_to_all | solution.py:262
  100.9 13.0 %all-to-all-start.3 = ((bf16[16,16,768]{2,1,0:T(8,128)(2,1)}), bf16[16,16,768]{2,1,0:T(8,128)(2,1)S(1)}, u32[]{:S(2)}, u32[]{:S(2)}) async-start(bf16[16,16,768]{2,1,0:T(8,128)(2,1)} %bitcast.46), calls=%async_computation.3 | async-start | bytes 786432 | tf_op jit(solution)/shard_map/all_to_all | solution.py:281
  116.5 11.7 %collective-permute-start.14 = (bf16[16,1024]{1,0:T(8,128)(2,1)}, bf16[16,1024]{1,0:T(8,128)(2,1)S(1)}, u32[]{:S(2)}, u32[]{:S(2)}) collective-permute-start(bf16[16,1024]{1,0:T(8,128)(2,1)} %get-tuple-element.34), channel_id=1, source_target_pairs={{0,7},{1,6},{2,5},{3,4},{4,3},{5,2},{6,1},{7,0},{8,15},{9,14},{10,... | collective-permute-start | bytes 98312 | tf_op jit(solution)/shard_map/ppermute | solution.py:285
  121.7 8.0 %collective-permute-start.13 = (bf16[16,1024]{1,0:T(8,128)(2,1)}, bf16[16,1024]{1,0:T(8,128)(2,1)S(1)}, u32[]{:S(2)}, u32[]{:S(2)}) collective-permute-start(bf16[16,1024]{1,0:T(8,128)(2,1)} %get-tuple-element.33), channel_id=1, source_target_pairs={{0,6},{1,7},{2,4},{3,5},{4,2},{5,3},{6,0},{7,1},{8,14},{9,15},{10,... | collective-permute-start | bytes 98312 | tf_op jit(solution)/shard_map/ppermute | solution.py:285
  122.1 8.0 %collective-permute-start.12 = (bf16[16,1024]{1,0:T(8,128)(2,1)}, bf16[16,1024]{1,0:T(8,128)(2,1)S(1)}, u32[]{:S(2)}, u32[]{:S(2)}) collective-permute-start(bf16[16,1024]{1,0:T(8,128)(2,1)} %get-tuple-element.32), channel_id=1, source_target_pairs={{0,5},{1,4},{2,7},{3,6},{4,1},{5,0},{6,3},{7,2},{8,13},{9,12},{10,... | collective-permute-start | bytes 98312 | tf_op jit(solution)/shard_map/ppermute | solution.py:285
  125.5 5.6 %collective-permute-start.11 = (bf16[16,1024]{1,0:T(8,128)(2,1)}, bf16[16,1024]{1,0:T(8,128)(2,1)S(1)}, u32[]{:S(2)}, u32[]{:S(2)}) collective-permute-start(bf16[16,1024]{1,0:T(8,128)(2,1)} %get-tuple-element.31), channel_id=1, source_target_pairs={{0,4},{1,5},{2,6},{3,7},{4,0},{5,1},{6,2},{7,3},{8,12},{9,13},{10,... | collective-permute-start | bytes 98312 | tf_op jit(solution)/shard_map/ppermute | solution.py:285
  126.0 5.5 %collective-permute-start.10 = (bf16[16,1024]{1,0:T(8,128)(2,1)}, bf16[16,1024]{1,0:T(8,128)(2,1)S(1)}, u32[]{:S(2)}, u32[]{:S(2)}) collective-permute-start(bf16[16,1024]{1,0:T(8,128)(2,1)} %get-tuple-element.30), channel_id=1, source_target_pairs={{0,3},{1,2},{2,1},{3,0},{4,7},{5,6},{6,5},{7,4},{8,11},{9,10},{10,... | collective-permute-start | bytes 98312 | tf_op jit(solution)/shard_map/ppermute | solution.py:285
  128.2 5.6 %collective-permute-start.9 = (bf16[16,1024]{1,0:T(8,128)(2,1)}, bf16[16,1024]{1,0:T(8,128)(2,1)S(1)}, u32[]{:S(2)}, u32[]{:S(2)}) collective-permute-start(bf16[16,1024]{1,0:T(8,128)(2,1)} %get-tuple-element.29), channel_id=1, source_target_pairs={{0,2},{1,3},{2,0},{3,1},{4,6},{5,7},{6,4},{7,5},{8,10},{9,11},{10,... | collective-permute-start | bytes 98312 | tf_op jit(solution)/shard_map/ppermute | solution.py:285
  129.7 4.1 %collective-permute-start.8 = (bf16[16,1024]{1,0:T(8,128)(2,1)}, bf16[16,1024]{1,0:T(8,128)(2,1)S(1)}, u32[]{:S(2)}, u32[]{:S(2)}) collective-permute-start(bf16[16,1024]{1,0:T(8,128)(2,1)} %get-tuple-element.28), channel_id=1, source_target_pairs={{0,1},{1,0},{2,3},{3,2},{4,5},{5,4},{6,7},{7,6},{8,9},{9,8},{10,11... | collective-permute-start | bytes 98312 | tf_op jit(solution)/shard_map/ppermute | solution.py:285
  (6 other events, 18.6 us)

commit v5 on v3

--- a/solution.py
+++ b/solution.py
@@ -86,13 +86,31 @@
     return mixed.astype(jnp.bfloat16).reshape(count, width_q)
 
 
-def project_body(q_ref, k_ref, v_ref, in_ref):
-    height = q_ref.shape[0]
-    qw, kw = q_ref.shape[1], k_ref.shape[1]
-    in_ref[0, 0:height, 0:qw] = q_ref[...].astype(jnp.bfloat16)
-    in_ref[0, 0:height, qw : qw + kw] = k_ref[...].astype(jnp.bfloat16)
-    in_ref[0, 0:height, qw + kw : qw + 2 * kw] = v_ref[...].astype(jnp.bfloat16)
-    in_ref[0, height:ROWS, :] = jnp.zeros((ROWS - height, qw + 2 * kw), jnp.bfloat16)
+def project_body(block_ref, in_ref, q_ref, k_ref, v_ref, sems):
+    slices, height, qw = q_ref.shape
+    kw = k_ref.shape[2]
+    copies = []
+    for t in range(slices):
+        sources = [
+            (t * qw, qw, q_ref),
+            (HQ * HD + t * kw, kw, k_ref),
+            ((HQ + KV) * HD + t * kw, kw, v_ref),
+        ]
+        for part, (column, width, target) in enumerate(sources):
+            copies.append(
+                pltpu.make_async_copy(
+                    block_ref.at[:, pl.ds(column, width)], target.at[t], sems.at[t, part]
+                )
+            )
+    for copy in copies:
+        copy.start()
+    for t in range(slices):
+        for copy in copies[3 * t : 3 * t + 3]:
+            copy.wait()
+        in_ref[t, 0:height, 0:qw] = q_ref[t].astype(jnp.bfloat16)
+        in_ref[t, 0:height, qw : qw + kw] = k_ref[t].astype(jnp.bfloat16)
+        in_ref[t, 0:height, qw + kw : qw + 2 * kw] = v_ref[t].astype(jnp.bfloat16)
+        in_ref[t, height:ROWS, :] = jnp.zeros((ROWS - height, qw + 2 * kw), jnp.bfloat16)
 
 
 def split_project(block, slices):
@@ -101,16 +119,17 @@
     kw = KV * HD // slices
     return pl.pallas_call(
         project_body,
-        grid=(slices,),
-        in_specs=[
-            pl.BlockSpec((height, qw), lambda t: (0, t)),
-            pl.BlockSpec((height, kw), lambda t: (0, HQ * HD // kw + t)),
-            pl.BlockSpec((height, kw), lambda t: (0, (HQ + KV) * HD // kw + t)),
+        in_specs=[pl.BlockSpec(memory_space=pl.ANY)],
+        out_specs=pl.BlockSpec(memory_space=pltpu.VMEM),
+        out_shape=jax.ShapeDtypeStruct((slices, ROWS, qw + 2 * kw), jnp.bfloat16),
+        scratch_shapes=[
+            pltpu.VMEM((slices, height, qw), jnp.float32),
+            pltpu.VMEM((slices, height, kw), jnp.float32),
+            pltpu.VMEM((slices, height, kw), jnp.float32),
+            pltpu.SemaphoreType.DMA((slices, 3)),
         ],
-        out_specs=pl.BlockSpec((1, ROWS, qw + 2 * kw), lambda t: (t, 0, 0)),
-        out_shape=jax.ShapeDtypeStruct((slices, ROWS, qw + 2 * kw), jnp.bfloat16),
         name="split_project",
-    )(block, block, block)
+    )(block)
 
 
 def output_body(o_ref, out_ref):

time: 133 us -> 131 us (0.985)
  Pallas kernels: 16.6 us -> 14.1 us
    pallas_call x1, Pallas kernels: 5.7 us -> 3.21 us  [split_project(): pl.pallas_call(project_body, in_specs=[pl.BlockSpec(memory_space=pl.ANY)]...]
  transfers between devices with their start and end apart: 11 -> 11, of which waited for: 2 -> 2; matrix products, arithmetic and copies ran while one was open for 13% -> 14% of each run, Pallas kernels for 7% -> 7%
where the time goes in v5:
time: 131 us; the launch traced here: 130 us
  blocking collectives  47 us (36%)
  starting transfers between devices  32 us (24%)
  matrix products  16 us (12%)
  Pallas kernels  14.1 us (11%)
  waiting for transfers between devices  12.5 us (10%)
  other arithmetic  4.1 us (3%)
  local copies, waits for them, and re-layouts  3.94 us (3%)
    all_gather x1, blocking collectives, body(): gathered = lax.all_gather(attended, 'replica', axis=0, tiled=True)  18.6 us
    all_to_all x1, blocking collectives, body(): lax.all_to_all(placed, 'tensor', split_axis=0, concat_axis=0, tiled=True)  15.7 us
    all_to_all x1, blocking collectives, body(): lax.all_to_all(parts, 'replica', split_axis=0, concat_axis=0, tiled=True)  12.7 us
    ppermute x8, starting transfers between devices, swap(): lax.ppermute(block, 'replica', [(m, m ^ step) for m in range(members)])  12.7 us
    all_to_all x1, waiting for transfers between devices, body(): lax.all_to_all(partial, 'replica', split_axis=0, concat_axis=0, tiled=True)  12.2 us
    all_to_all x1, starting transfers between devices, body(): lax.all_to_all(output_rows, 'tensor', split_axis=0, concat_axis=0, tiled=...  7.81 us
    all_to_all x1, starting transfers between devices, body(): lax.all_to_all(project_rows, 'tensor', split_axis=0, concat_axis=0, tiled...  7.16 us
    dot_general x1, matrix products, attend(): jnp.einsum('bskgd,bkcd->bkgsc', query, keys_cache, preferred_element_type...  5.82 us
  transfers between devices with their start and end apart: 11, of which 2 were waited for; matrix products, arithmetic and copies ran while one was open for 14% of the time, Pallas kernels for 7%

profile of v5, /device:TPU:0, one launch (start us, length us, event | category | flops | bytes accessed | tf_op | source)
XLA Modules:
  0.0 130.0 jit_solution(8461309480297022378)
XLA Ops:
  0.0 3.2 %split_project.1 = bf16[8,72,1280]{2,1,0:T(8,128)(2,1)} custom-call(f32[68,18432]{1,0:T(8,128)} %o_ref), custom_call_target="tpu_custom_call" | custom-call | tf_op jit(solution)/shard_map/split_project/pallas_call | solution.py:120
  3.3 7.2 %all-to-all-start = ((bf16[8,72,1280]{2,1,0:T(8,128)(2,1)}), bf16[8,72,1280]{2,1,0:T(8,128)(2,1)S(1)}, u32[]{:S(2)}, u32[]{:S(2)}) async-start(bf16[8,72,1280]{2,1,0:T(8,128)(2,1)} %split_project.1), calls=%async_computation | async-start | bytes 2949120 | tf_op jit(solution)/shard_map/all_to_all | solution.py:247
  11.6 0.8 reshape.336.tokens_ref
  12.4 1.7 %token_windows.1 = (bf16[8,16,768]{2,1,0:T(8,128)(2,1)}, bf16[8,16,768]{2,1,0:T(8,128)(2,1)}) custom-call(s32[16]{0:T(128)} %multiply_minimum_fusion.first_ref, s32[1]{0:T(128)} %bitcast.1.mine_ref, bf16[16,8192]{1,0:T(8,128)(2,1)} %reshape.336.tokens_ref), custom_call_target="tpu_custom_call" | custom-call | tf_op jit(solution)/shard_map/token_windows/pallas_call | solution.py:166
  14.2 1.2 dynamic_slice.13
  15.8 1.5 %fusion.40 = (bf16[2,16,768]{2,1,0:T(8,128)(2,1)S(1)}, bf16[2,16,768]{2,1,0:T(8,128)(2,1)}, bf16[2,16,768]{2,1,0:T(8,128)(2,1)S(1)}, bf16[2,16,768]{2,1,0:T(8,12...) fusion(bf16[8,1,16,768]{3,2,1,0:T(8,128)(2,1)S(1)} %bitcast.119, ...), kind=kLoop, calls=%fused_computation.55 | loop fusion | flops 196608 | bytes 786432 | tf_op jit(solution)/shard_map/squeeze | solution.py:206
  17.3 1.9 %collective-permute-start.1 = (bf16[2,16,768]{2,1,0:T(8,128)(2,1)S(1)}, bf16[2,16,768]{2,1,0:T(8,128)(2,1)S(1)}, u32[]{:S(2)}, u32[]{:S(2)}) collective-permute-start(bf16[2,16,768]{2,1,0:T(8,128)(2,1)S(1)} %get-tuple-element.21), channel_id=1, source_target_pairs={{0,16},{8,24},{16,0},{24,8},{32,48},{40,56},{48,32},{56,40},{64,80... | collective-permute-start | bytes 147464 | tf_op jit(solution)/shard_map/ppermute | solution.py:203
  19.2 3.6 %collective-permute-start.2 = (bf16[2,16,768]{2,1,0:T(8,128)(2,1)S(1)}, bf16[2,16,768]{2,1,0:T(8,128)(2,1)S(1)}, u32[]{:S(2)}, u32[]{:S(2)}) collective-permute-start(bf16[2,16,768]{2,1,0:T(8,128)(2,1)S(1)} %get-tuple-element.22), channel_id=1, source_target_pairs={{0,32},{8,40},{16,48},{24,56},{32,0},{40,8},{48,16},{56,24},{64,96... | collective-permute-start | bytes 147464 | tf_op jit(solution)/shard_map/ppermute | solution.py:203
  23.5 0.8 collective-permute-start.4
  24.9 4.9 %collective-permute-start.6 = (bf16[2,16,768]{2,1,0:T(8,128)(2,1)S(1)}, bf16[2,16,768]{2,1,0:T(8,128)(2,1)S(1)}, u32[]{:S(2)}, u32[]{:S(2)}) collective-permute-start(bf16[2,16,768]{2,1,0:T(8,128)(2,1)S(1)} %get-tuple-element.26), channel_id=1, source_target_pairs={{0,96},{8,104},{16,112},{24,120},{32,64},{40,72},{48,80},{56,88},{... | collective-permute-start | bytes 147464 | tf_op jit(solution)/shard_map/ppermute | solution.py:203
  29.7 0.9 collective-permute-start.7
  30.7 5.5 %split_output.1 = bf16[8,72,1024]{2,1,0:T(8,128)(2,1)} custom-call(f32[68,18432]{1,0:T(8,128)} %o_ref), custom_call_target="tpu_custom_call" | custom-call | tf_op jit(solution)/shard_map/split_output/pallas_call | solution.py:145
  37.2 1.8 %order_parts.1 = bf16[16,16,768]{2,1,0:T(8,128)(2,1)} custom-call(s32[1]{0:T(128)} %bitcast.1.mine_ref, bf16[2,16,768]{2,1,0:T(8,128)(2,1)} %get-tuple-element.20.refs_0_, bf16[2,16,768]{2,1,0:T(8,128)(2,1)} %copy-done.1, bf16[2,16,768]{2,1,0:T(8,128)(2,1)} %copy-done.2, bf16[2,16,768]{2,1,0:T(8,128)(2,1)} %copy-done.3, bf16[2,16,768]{2,1,0:T(8,128)(2,1)} %copy-done.4, ...), custom_call_target="tpu_custom_call" | custom-call | tf_op jit(solution)/shard_map/order_parts/pallas_call | solution.py:189
  38.9 3.0 %convolution_convert_fusion = bf16[256,1280]{1,0:T(8,128)(2,1)} fusion(bf16[576,1280]{1,0:T(8,128)(2,1)S(1)} %bitcast.113, bf16[256,768]{1,0:T(8,128)(2,1)} %bitcast.117, s32[576]{0:T(1024)S(1)} %select_n.37), kind=kOutput, calls=%fused_computation.8 | convolution fusion | flops 604897280 | bytes 2525440 | tf_op jit(solution)/shard_map/dot_general | solution.py:277
  41.9 4.4 %all-to-all-start.1 = ((bf16[16,16,1280]{2,1,0:T(8,128)(2,1)}), bf16[16,16,1280]{2,1,0:T(8,128)(2,1)S(1)}, u32[]{:S(2)}, u32[]{:S(2)}) async-start(bf16[16,16,1280]{2,1,0:T(8,128)(2,1)} %bitcast.17), calls=%async_computation.1 | async-start | bytes 1310720 | tf_op jit(solution)/shard_map/all_to_all | solution.py:279
  46.4 12.2 %all-to-all-done.1 = bf16[16,16,1280]{2,1,0:T(8,128)(2,1)S(1)} async-done(((bf16[16,16,1280]{2,1,0:T(8,128)(2,1)}), bf16[16,16,1280]{2,1,0:T(8,128)(2,1)S(1)}, u32[]{:S(2)}, u32[]{:S(2)}) %all-to-all-start.1) | async-done | bytes 655392 | tf_op jit(solution)/shard_map/all_to_all | solution.py:279
  58.6 7.8 %all-to-all-start.2 = ((bf16[8,72,1024]{2,1,0:T(8,128)(2,1)}), bf16[8,72,1024]{2,1,0:T(8,128)(2,1)S(1)}, u32[]{:S(2)}, u32[]{:S(2)}) async-start(bf16[8,72,1024]{2,1,0:T(8,128)(2,1)} %split_output.1), calls=%async_computation.2 | async-start | bytes 2359296 | tf_op jit(solution)/shard_map/all_to_all | solution.py:270
  66.8 5.8 %fusion.63 = (f32[8,8,2]{1,2,0:T(2,128)S(1)}, f32[8,1,8,2,4096]{4,2,3,0,1:T(8,128)S(1)}) fusion(bf16[8,1,4096,128]{3,2,1,0:T(8,128)(2,1)} %param.9, bf16[8,2,8,64]{3,2,1,0:T(8,128)(2,1)S(1)} %bitcast.122, bf16[8,2,8,64]{3,2,1,0:T(8,128)(2,1)S(1)} %bitcast.120, pred[8,4096]{1,0:T(8,128)(4,1)S(1)} %iota_compare_fusion.11), kind=kOutput, calls=%fused_computation.102 | convolution fusion | flops 135856000 | bytes 10551808 | tf_op jit(solution)/shard_map/bskgd,bkcd->bkgsc/dot_general | solution.py:64
  73.5 4.7 %fusion.21 = f32[8,128,8,2]{1,2,3,0:T(8,128)S(1)} fusion(bf16[8,1,4096,128]{3,2,1,0:T(8,128)(2,1)} %param.10, f32[8,1,8,2,4096]{4,2,3,0,1:T(8,128)S(1)} %get-tuple-element.34, f32[8,8,2]{1,2,0:T(2,128)S(1)} %add.74, f32[8,8,2]{1,2,0:T(2,128)S(1)} %max.9), kind=kOutput, calls=%fused_computation.19 | convolution fusion | flops 135790592 | bytes 10552320 | tf_op jit(solution)/shard_map/bkgsc,bkcd->bskgd/dot_general | solution.py:80
  78.5 18.6 %all_gather.3 = bf16[256,1024]{1,0:T(8,128)(2,1)S(1)} all-gather(bf16[16,1024]{1,0:T(8,128)(2,1)S(1)} %bitcast.124), channel_id=1, replica_groups=mesh['replica'=16,'tensor'=8] {'replica'}, dimensions={0}, use_global_device_ids=true | all-gather | bytes 557056 | tf_op jit(solution)/shard_map/all_gather | solution.py:289
  97.1 1.9 %convolution_convert_fusion.1 = bf16[256,768]{1,0:T(8,128)(2,1)S(1)} fusion(bf16[256,1024]{1,0:T(8,128)(2,1)S(1)} %all_gather.3, bf16[576,1024]{1,0:T(8,128)(2,1)S(1)} %bitcast.114, s32[576]{0:T(1024)S(1)} %select_n.37), kind=kOutput, calls=%fused_computation.17 | convolution fusion | flops 1310048256 | bytes 2099456 | tf_op jit(solution)/shard_map/dot_general | solution.py:293
  98.9 12.7 %all_to_all.25.part_ref = bf16[16,16,768]{2,1,0:T(8,128)(2,1)} all-to-all(bf16[16,16,768]{2,1,0:T(8,128)(2,1)S(1)} %bitcast.116), channel_id=1, replica_groups=mesh['replica'=16,'tensor'=8] {'replica'}, dimensions={0} | all-to-all | bytes 786432 | tf_op jit(solution)/shard_map/all_to_all | solution.py:297
  111.7 1.9 %place_windows.1 = bf16[8,16,1024]{2,1,0:T(8,128)(2,1)} custom-call(s32[16]{0:T(128)} %multiply_minimum_fusion.first_ref, bf16[16,16,768]{2,1,0:T(8,128)(2,1)} %all_to_all.25.part_ref), custom_call_target="tpu_custom_call" | custom-call | tf_op jit(solution)/shard_map/place_windows/pallas_call | solution.py:224
  113.6 15.7 %all_to_all.26 = bf16[8,16,1024]{2,1,0:T(8,128)(2,1)S(1)} all-to-all(bf16[8,16,1024]{2,1,0:T(8,128)(2,1)} %place_windows.1), channel_id=1, replica_groups=mesh['replica'=16,'tensor'=8] {'tensor'}, dimensions={0} | all-to-all | bytes 524288 | tf_op jit(solution)/shard_map/all_to_all | solution.py:299
  (67 shorter events, 6.0 us)
Async XLA Ops:
  3.2 7.2 %copy-start.8 = (s32[128]{0:T(128)S(1)}, s32[128]{0:T(128)}, u32[]{:S(2)}) copy-start(s32[128]{0:T(128)} %param.8) | copy-start | bytes 1540
  3.2 8.3 %copy-start = (bf16[8,2,8192]{2,1,0:T(2,128)(2,1)S(1)}, bf16[8,2,8192]{2,1,0:T(2,128)(2,1)}, u32[]{:S(2)}) copy-start(bf16[8,2,8192]{2,1,0:T(2,128)(2,1)} %param.6) | copy-start | bytes 786436
  3.2 12.2 %copy-start.9 = (s32[8]{0:T(128)S(1)}, s32[8]{0:T(128)}, u32[]{:S(2)}) copy-start(s32[8]{0:T(128)} %param.11) | copy-start | bytes 100
  3.3 35.7 %all-to-all-start = ((bf16[8,72,1280]{2,1,0:T(8,128)(2,1)}), bf16[8,72,1280]{2,1,0:T(8,128)(2,1)S(1)}, u32[]{:S(2)}, u32[]{:S(2)}) async-start(bf16[8,72,1280]{2,1,0:T(8,128)(2,1)} %split_project.1), calls=%async_computation | async-start | bytes 2949120 | tf_op jit(solution)/shard_map/all_to_all | solution.py:247
  14.1 1.7 %collective-permute-start = (bf16[8,16,768]{2,1,0:T(8,128)(2,1)}, bf16[8,16,768]{2,1,0:T(8,128)(2,1)S(1)}, u32[]{:S(2)}, u32[]{:S(2)}) collective-permute-start(bf16[8,16,768]{2,1,0:T(8,128)(2,1)} %get-tuple-element.16), channel_id=1, source_target_pairs={{0,8},{8,0},{16,24},{24,16},{32,40},{40,32},{48,56},{56,48},{64,72... | collective-permute-start | bytes 589832 | tf_op jit(solution)/shard_map/ppermute | solution.py:203
  17.3 7.6 %collective-permute-start.1 = (bf16[2,16,768]{2,1,0:T(8,128)(2,1)S(1)}, bf16[2,16,768]{2,1,0:T(8,128)(2,1)S(1)}, u32[]{:S(2)}, u32[]{:S(2)}) collective-permute-start(bf16[2,16,768]{2,1,0:T(8,128)(2,1)S(1)} %get-tuple-element.21), channel_id=1, source_target_pairs={{0,16},{8,24},{16,0},{24,8},{32,48},{40,56},{48,32},{56,40},{64,80... | collective-permute-start | bytes 147464 | tf_op jit(solution)/shard_map/ppermute | solution.py:203
  19.2 10.5 %collective-permute-start.2 = (bf16[2,16,768]{2,1,0:T(8,128)(2,1)S(1)}, bf16[2,16,768]{2,1,0:T(8,128)(2,1)S(1)}, u32[]{:S(2)}, u32[]{:S(2)}) collective-permute-start(bf16[2,16,768]{2,1,0:T(8,128)(2,1)S(1)} %get-tuple-element.22), channel_id=1, source_target_pairs={{0,32},{8,40},{16,48},{24,56},{32,0},{40,8},{48,16},{56,24},{64,96... | collective-permute-start | bytes 147464 | tf_op jit(solution)/shard_map/ppermute | solution.py:203
  23.4 12.8 %collective-permute-start.3 = (bf16[2,16,768]{2,1,0:T(8,128)(2,1)S(1)}, bf16[2,16,768]{2,1,0:T(8,128)(2,1)S(1)}, u32[]{:S(2)}, u32[]{:S(2)}) collective-permute-start(bf16[2,16,768]{2,1,0:T(8,128)(2,1)S(1)} %get-tuple-element.23), channel_id=1, source_target_pairs={{0,48},{8,56},{16,32},{24,40},{32,16},{40,24},{48,0},{56,8},{64,11... | collective-permute-start | bytes 147464 | tf_op jit(solution)/shard_map/ppermute | solution.py:203
  23.5 12.7 %collective-permute-start.4 = (bf16[2,16,768]{2,1,0:T(8,128)(2,1)S(1)}, bf16[2,16,768]{2,1,0:T(8,128)(2,1)S(1)}, u32[]{:S(2)}, u32[]{:S(2)}) collective-permute-start(bf16[2,16,768]{2,1,0:T(8,128)(2,1)S(1)} %get-tuple-element.24), channel_id=1, source_target_pairs={{0,64},{8,72},{16,80},{24,88},{32,96},{40,104},{48,112},{56,120},{... | collective-permute-start | bytes 147464 | tf_op jit(solution)/shard_map/ppermute | solution.py:203
  24.2 12.0 %collective-permute-start.5 = (bf16[2,16,768]{2,1,0:T(8,128)(2,1)S(1)}, bf16[2,16,768]{2,1,0:T(8,128)(2,1)S(1)}, u32[]{:S(2)}, u32[]{:S(2)}) collective-permute-start(bf16[2,16,768]{2,1,0:T(8,128)(2,1)S(1)} %get-tuple-element.25), channel_id=1, source_target_pairs={{0,80},{8,88},{16,64},{24,72},{32,112},{40,120},{48,96},{56,104},{... | collective-permute-start | bytes 147464 | tf_op jit(solution)/shard_map/ppermute | solution.py:203
  24.9 11.3 %copy-start.1 = (bf16[2,16,768]{2,1,0:T(8,128)(2,1)}, bf16[2,16,768]{2,1,0:T(8,128)(2,1)S(1)}, u32[]{:S(2)}) copy-start(bf16[2,16,768]{2,1,0:T(8,128)(2,1)S(1)} %collective-permute-done.1.refs_1_) | copy-start | bytes 147460
  24.9 11.4 %collective-permute-start.6 = (bf16[2,16,768]{2,1,0:T(8,128)(2,1)S(1)}, bf16[2,16,768]{2,1,0:T(8,128)(2,1)S(1)}, u32[]{:S(2)}, u32[]{:S(2)}) collective-permute-start(bf16[2,16,768]{2,1,0:T(8,128)(2,1)S(1)} %get-tuple-element.26), channel_id=1, source_target_pairs={{0,96},{8,104},{16,112},{24,120},{32,64},{40,72},{48,80},{56,88},{... | collective-permute-start | bytes 147464 | tf_op jit(solution)/shard_map/ppermute | solution.py:203
  29.7 6.5 %copy-start.2 = (bf16[2,16,768]{2,1,0:T(8,128)(2,1)}, bf16[2,16,768]{2,1,0:T(8,128)(2,1)S(1)}, u32[]{:S(2)}) copy-start(bf16[2,16,768]{2,1,0:T(8,128)(2,1)S(1)} %collective-permute-done.2.refs_2_) | copy-start | bytes 147460
  29.7 6.8 %collective-permute-start.7 = (bf16[2,16,768]{2,1,0:T(8,128)(2,1)S(1)}, bf16[2,16,768]{2,1,0:T(8,128)(2,1)S(1)}, u32[]{:S(2)}, u32[]{:S(2)}) collective-permute-start(bf16[2,16,768]{2,1,0:T(8,128)(2,1)S(1)} %get-tuple-element.19), channel_id=1, source_target_pairs={{0,112},{8,120},{16,96},{24,104},{32,80},{40,88},{48,64},{56,72},{... | collective-permute-start | bytes 147464 | tf_op jit(solution)/shard_map/ppermute | solution.py:203
  36.2 0.6 copy-start.3
  36.2 0.6 copy-start.4
  36.2 0.6 copy-start.5
  36.3 0.6 copy-start.6
  36.5 0.6 copy-start.7
  41.9 16.7 %all-to-all-start.1 = ((bf16[16,16,1280]{2,1,0:T(8,128)(2,1)}), bf16[16,16,1280]{2,1,0:T(8,128)(2,1)S(1)}, u32[]{:S(2)}, u32[]{:S(2)}) async-start(bf16[16,16,1280]{2,1,0:T(8,128)(2,1)} %bitcast.17), calls=%async_computation.1 | async-start | bytes 1310720 | tf_op jit(solution)/shard_map/all_to_all | solution.py:279
  58.6 38.5 %all-to-all-start.2 = ((bf16[8,72,1024]{2,1,0:T(8,128)(2,1)}), bf16[8,72,1024]{2,1,0:T(8,128)(2,1)S(1)}, u32[]{:S(2)}, u32[]{:S(2)}) async-start(bf16[8,72,1024]{2,1,0:T(8,128)(2,1)} %split_output.1), calls=%async_computation.2 | async-start | bytes 2359296 | tf_op jit(solution)/shard_map/all_to_all | solution.py:270
